TPU v7x, 32 devices: a whole 2x2x4 slice. The times are simulated.
32 devices in a mesh: space: 16 (over z, x, core), batch: 2 (over y).
Axes of the slice: x: 2, y: 2, z: 4, core: 2. Of those that a mesh axis runs over, the one named last changes fastest.
Arguments:
- fine_parts: bfloat16 [2, 8192, 128], P('batch', 'space'), may hold values from -6 to 6
- parent_parts: bfloat16 [2, 1024, 128], P('batch', 'space'), may hold values from -6 to 6
- coarse_local: float32 [1024, 128], P('space'), may hold values from -6 to 6
- fine_source: int32 [189, 8192], P(None, 'space'), may hold values from 0 to 159
- fine_operator: int32 [189, 8192], P(None, 'space'), may hold values from 0 to 63
- parent_source: int32 [189, 1024], P(None, 'space'), may hold values from 0 to 159
- parent_operator: int32 [189, 1024], P(None, 'space'), may hold values from 0 to 63
- operators: bfloat16 [64, 128, 128], replicated, may hold values from -0.0390625 to 0.0390625
- child_shift: bfloat16 [8, 128, 128], replicated, may hold values from -0.5 to 0.5
- basis: bfloat16 [8192, 32, 128], P('space', 'batch'), may hold values from -0.5 to 0.5
- counts: int32 [2, 8192], P('batch', 'space'), may hold values from 1 to 16
Outputs:
- potential: float32 [32, 8192], P('batch', 'space')
Inputs may be any that keep to these rules, and one draw needn't show every extreme that they name: `fine_source`: an entry v names, in the target's own block if v // 32 is 0 and else in the block whose index differs from the target's in bit v // 32 - 1, box v % 32 of the aligned group of 32 boxes that holds the target's position. `parent_source`: an entry v names, in the target's own block if v // 32 is 0 and else in the block whose index differs from the target's in bit v // 32 - 1, parent box v % 32 of the aligned group of 32 parent boxes that holds the target's position.
All inputs are finite; a program needn't handle non-finite values.
Results may differ from a plain program's by a relative error of at most 0.015.
Values may be sent and summed in bfloat16 or wider, within the bound.
No kernel may reach another device: no remote copies, remote signals or barrier semaphores. Data moves between devices by JAX's collectives and lax.ppermute only.
A program may use at most 64 MiB of HBM per device.

v0:
```python
import math

import jax
import jax.numpy as jnp
from jax import lax
from jax.sharding import PartitionSpec as P

NTERMS = 121
WINDOW = 32


def partner(shard, axis, apart):
    return lax.ppermute(shard, axis, [(i, i ^ 1 << apart) for i in range(lax.axis_size(axis))])


def far_field(stacked, source_list, operator_list, operators, row_start):
    kind_count, coef_width, _ = operators.shape
    flat_ops = operators.reshape(kind_count * coef_width, coef_width)
    list_length, total_rows = source_list.shape
    piece_rows = math.gcd(total_rows, WINDOW)
    piece_count = total_rows // piece_rows
    source_pieces = source_list.reshape(list_length, piece_count, piece_rows).transpose(1, 0, 2)
    kind_pieces = operator_list.reshape(list_length, piece_count, piece_rows).transpose(1, 0, 2)
    starts = row_start + lax.iota(jnp.int32, piece_count) * piece_rows
    kinds_iota = lax.iota(jnp.int32, kind_count)
    column_iota = lax.iota(jnp.int32, stacked.shape[0] * WINDOW)

    def one_piece(pieces):
        sources, kinds, start = pieces
        corner = start // WINDOW * WINDOW
        nearby = lax.dynamic_slice_in_dim(stacked, corner, WINDOW, 1).reshape(-1, coef_width)
        chosen = (sources[:, :, None] == column_iota).astype(jnp.bfloat16)
        onehot = (kinds[:, :, None] == kinds_iota).astype(jnp.bfloat16)
        counted = jnp.einsum(
            "jbt,jbr->btr", onehot, chosen, preferred_element_type=jnp.float32
        ).astype(jnp.bfloat16)
        grouped = jnp.einsum(
            "btr,rk->btk", counted, nearby, preferred_element_type=jnp.float32
        ).astype(jnp.bfloat16)
        return jnp.dot(
            grouped.reshape(piece_rows, kind_count * coef_width),
            flat_ops,
            preferred_element_type=jnp.float32,
        )

    return lax.map(one_piece, (source_pieces, kind_pieces, starts)).reshape(total_rows, coef_width)


def with_partners(fine_mult, parent_mult):
    fine_blocks = [fine_mult]
    parent_blocks = [parent_mult]
    for bit_number in range(4):
        fine_other, parent_other = partner((fine_mult, parent_mult), "space", bit_number)
        fine_blocks.append(fine_other)
        parent_blocks.append(parent_other)
    return (jnp.stack(fine_blocks), jnp.stack(parent_blocks))


def children(parent_local, fine_far, child_shift):
    shifted = jnp.einsum(
        "pk,okl->pol", parent_local, child_shift, preferred_element_type=jnp.float32
    )
    whole = shifted.reshape(fine_far.shape) + fine_far
    keep = lax.iota(jnp.int32, whole.shape[1]) < NTERMS
    return jnp.where(keep[None, :], whole, 0.0).astype(jnp.bfloat16)


def body(
    fine_parts,
    parent_parts,
    coarse_local,
    fine_source,
    fine_operator,
    parent_source,
    parent_operator,
    operators,
    child_shift,
    basis,
    counts,
):
    fine_terms = fine_parts[0].astype(jnp.float32)
    parent_terms = parent_parts[0].astype(jnp.float32)
    group_size = lax.axis_size("batch")
    member = lax.axis_index("batch")
    fine_share, parent_share = (
        lax.psum_scatter(
            fine_terms.astype(jnp.bfloat16), "batch", scatter_dimension=0, tiled=True
        ).astype(jnp.float32),
        lax.psum_scatter(
            parent_terms.astype(jnp.bfloat16), "batch", scatter_dimension=0, tiled=True
        ).astype(jnp.float32),
    )
    fine_pieces, parent_pieces = with_partners(
        fine_share.astype(jnp.bfloat16), parent_share.astype(jnp.bfloat16)
    )
    fine_stack, parent_stack = (
        lax.all_gather(fine_pieces, "batch", axis=1, tiled=True),
        lax.all_gather(parent_pieces, "batch", axis=1, tiled=True),
    )
    fine_width = fine_source.shape[1] // group_size
    parent_width = parent_source.shape[1] // group_size
    my_fine_source = lax.dynamic_slice_in_dim(fine_source, member * fine_width, fine_width, 1)
    my_fine_kinds = lax.dynamic_slice_in_dim(fine_operator, member * fine_width, fine_width, 1)
    my_parent_source = lax.dynamic_slice_in_dim(
        parent_source, member * parent_width, parent_width, 1
    )
    my_parent_kinds = lax.dynamic_slice_in_dim(
        parent_operator, member * parent_width, parent_width, 1
    )
    coarse_share = lax.dynamic_slice_in_dim(coarse_local, member * parent_width, parent_width, 0)
    fine_far = far_field(fine_stack, my_fine_source, my_fine_kinds, operators, member * fine_width)
    parent_far = far_field(
        parent_stack, my_parent_source, my_parent_kinds, operators, member * parent_width
    )
    parent_local = (coarse_share + parent_far).astype(jnp.bfloat16)
    local_share = children(parent_local, fine_far, child_shift)
    local = lax.all_gather(local_share, "batch", axis=0, tiled=True)
    values = lax.dot_general(
        basis, local, (((2,), (1,)), ((0,), (0,))), preferred_element_type=jnp.float32
    ).T
    slot_index = lax.iota(jnp.int32, values.shape[0])[:, None]
    return jnp.where(slot_index < counts, values, 0.0)


def solution(mesh):
    placed = (
        P("batch", "space", None),
        P("batch", "space", None),
        P("space", None),
        P(None, "space"),
        P(None, "space"),
        P(None, "space"),
        P(None, "space"),
        P(),
        P(),
        P("space", "batch", None),
        P("batch", "space"),
    )
    return jax.shard_map(
        body, mesh=mesh, in_specs=placed, out_specs=P("batch", "space"), check_vma=False
    )
```

profile of v0, /device:TPU:0, one launch (start us, length us, event | category | flops | bytes accessed | tf_op | source)
XLA Modules:
  0.0 194.0 jit_solution(10748365135499248731)
XLA Ops:
  10.3 2.4 %iota_compare_fusion.2 = pred[189,32,160]{2,1,0:T(32,128)(4,1)} fusion(s32[189,32]{1,0:T(8,128)S(1)} %copy.15), kind=kLoop, calls=%fused_computation.19 | loop fusion | flops 967680 | bytes 991872 | tf_op jit(solution)/shard_map/while/body/eval_jaxpr/eq | solution.py:32
  12.8 1.5 iota_compare_fusion.3
  14.2 8.0 %reduce-scatter.3.cloned.1.call-done = bf16[32,128]{1,0:T(8,128)(2,1)} async-done(((bf16[64,128]{1,0:T(8,128)(2,1)}), bf16[32,128]{1,0:T(8,128)(2,1)}) %reduce-scatter.3.cloned.1.call-update) | async-done | bytes 8208 | tf_op jit(solution)/shard_map/reduce_scatter | solution.py:89
  22.9 1.5 collective-permute-start.1
  24.4 1.5 collective-permute-start.2
  25.9 2.4 %collective-permute-start.3 = (bf16[32,128]{1,0:T(8,128)(2,1)}, bf16[32,128]{1,0:T(8,128)(2,1)S(1)}, u32[]{:S(2)}, u32[]{:S(2)}) collective-permute-start(bf16[32,128]{1,0:T(8,128)(2,1)} %reduce-scatter.3.cloned.1.call-done), channel_id=1, source_target_pairs={{0,16},{2,18},{4,20},{6,22},{8,24},{10,26},{12,28},{14,30},{16,0},... | collective-permute-start | bytes 24584 | tf_op jit(solution)/shard_map/ppermute | solution.py:13
  28.3 2.4 %collective-permute-done.3 = bf16[32,128]{1,0:T(8,128)(2,1)S(1)} collective-permute-done((bf16[32,128]{1,0:T(8,128)(2,1)}, bf16[32,128]{1,0:T(8,128)(2,1)S(1)}, u32[]{:S(2)}, u32[]{:S(2)}) %collective-permute-start.3) | collective-permute-done | bytes 8224 | tf_op jit(solution)/shard_map/ppermute | solution.py:13
  30.7 4.7 %all_gather.9 = bf16[5,64,128]{2,1,0:T(8,128)(2,1)S(1)} all-gather(bf16[5,32,128]{2,1,0:T(8,128)(2,1)S(1)} %constant_dynamic-update-slice_fusion), channel_id=1, replica_groups=mesh['space'=16,'batch'=2] {'batch'}, dimensions={1}, use_global_device_ids=true | all-gather | bytes 122880 | tf_op jit(solution)/shard_map/all_gather | solution.py:98
  35.4 4.7 %fusion.38 = bf16[32,64,128]{2,1,0:T(8,128)(2,1)} fusion(bf16[160,128,1]{1,0,2:T(8,128)(2,1)S(1)} %bitcast.107, pred[189,32,160]{2,1,0:T(32,128)(4,1)} %iota_compare_fusion.2, pred[189,32,64]{2,1,0:T(32,128)(4,1)S(1)} %iota_compare_fusion.3), kind=kOutput, calls=%fused_computation.24 | convolution fusion | flops 208338944 | bytes 1920000 | tf_op jit(solution)/shard_map/while/body/eval_jaxpr/btr,rk->btk/dot_general | solution.py:37
  40.1 3.1 %fusion.46 = f32[32,8,128]{2,0,1:T(8,128)} fusion(bf16[8,128,128]{2,1,0:T(8,128)(2,1)} %param.21, bf16[64,128,128]{2,1,0:T(8,128)(2,1)} %param.20, bf16[32,64,128]{2,1,0:T(8,128)(2,1)} %fusion.38, f32[64,128]{1,0:T(8,128)S(1)} %copy-done.5, s32[]{:T(128)S(6)} %select_n.39), kind=kOutput, calls=%fused_computation.29 | convolution fusion | flops 75505664 | bytes 3031044 | tf_op jit(solution)/shard_map/pk,okl->pol/dot_general | solution.py:60
  45.6 2.4 %collective-permute-start.7 = (bf16[256,128]{1,0:T(8,128)(2,1)}, bf16[256,128]{1,0:T(8,128)(2,1)S(1)}, u32[]{:S(2)}, u32[]{:S(2)}) collective-permute-start(bf16[256,128]{1,0:T(8,128)(2,1)} %reduce-scatter.5.cloned.1.call-done), channel_id=1, source_target_pairs={{0,16},{2,18},{4,20},{6,22},{8,24},{10,26},{12,28},{14,30},{16,0},... | collective-permute-start | bytes 196616 | tf_op jit(solution)/shard_map/ppermute | solution.py:13
  49.1 2.5 %collective-permute-done.7 = bf16[256,128]{1,0:T(8,128)(2,1)S(1)} collective-permute-done((bf16[256,128]{1,0:T(8,128)(2,1)}, bf16[256,128]{1,0:T(8,128)(2,1)S(1)}, u32[]{:S(2)}, u32[]{:S(2)}) %collective-permute-start.7) | collective-permute-done | bytes 65568 | tf_op jit(solution)/shard_map/ppermute | solution.py:13
  51.6 8.6 %all_gather.10 = bf16[5,512,128]{2,1,0:T(8,128)(2,1)} all-gather(bf16[5,256,128]{2,1,0:T(8,128)(2,1)S(1)} %bitcast_dynamic-update-slice_fusion), channel_id=1, replica_groups=mesh['space'=16,'batch'=2] {'batch'}, dimensions={1}, use_global_device_ids=true | all-gather | bytes 983040 | tf_op jit(solution)/shard_map/all_gather | solution.py:97
  60.2 119.0 %while.17 = (s32[]{:T(128)}, f32[8,32,128]{2,1,0:T(8,128)}, s32[8,189,32]{1,2,0:T(8,128)S(1)}, s32[8,189,32]{1,2,0:T(8,128)S(1)}, s32[8]{0:T(128)S(1)}, /*index=...) while((s32[]{:T(128)}, f32[8,32,128]{2,1,0:T(8,128)}, ...), condition=%wide.region_3.4_spmd.clone, body=%wide.region_2.3_spmd.clone.sunk | while | flops 276802560 | bytes 9333465 | solution.py:46
  64.3 2.4 %iota_compare_fusion.8 = pred[189,32,160]{2,1,0:T(32,128)(4,1)} fusion(s32[189,32]{1,0:T(8,128)S(1)} %bitcast.100), kind=kLoop, calls=%fused_computation.4.clone.1 | loop fusion | flops 967680 | bytes 991872 | tf_op jit(solution)/shard_map/while/body/eval_jaxpr/eq | solution.py:32
  66.8 1.5 iota_compare_fusion.9
  68.3 3.9 %fusion.73 = bf16[32,64,128]{2,1,0:T(8,128)(2,1)S(1)} fusion(bf16[160,128,1]{1,0,2:T(8,128)(2,1)S(1)} %bitcast.102, pred[189,32,160]{2,1,0:T(32,128)(4,1)} %iota_compare_fusion.8, pred[189,32,64]{2,1,0:T(32,128)(4,1)S(1)} %iota_compare_fusion.9), kind=kOutput, calls=%fused_computation.9.clone.1 | convolution fusion | flops 208338944 | bytes 1920000 | tf_op jit(solution)/shard_map/while/body/eval_jaxpr/btr,rk->btk/dot_general | solution.py:37
  72.3 2.8 %fusion.74 = f32[8,32,128]{2,1,0:T(8,128)} fusion(f32[8,32,128]{2,1,0:T(8,128)} %get-tuple-element.253, s32[]{:T(128)S(6)} %copy.92, bf16[8192,128]{1,0:T(8,128)(2,1)} %get-tuple-element.272, bf16[4,8,64,128]{3,2,1,0:T(8,128)(2,1)S(1)} %bitcast.99), kind=kOutput, calls=%fused_computation.11.clone.1 | convolution fusion | flops 67108864 | bytes 2637828 | tf_op jit(solution)/shard_map/while/body/eval_jaxpr/dot_general | solution.py:40
  79.2 2.4 %iota_compare_fusion.8 = pred[189,32,160]{2,1,0:T(32,128)(4,1)} fusion(s32[189,32]{1,0:T(8,128)S(1)} %bitcast.100), kind=kLoop, calls=%fused_computation.4.clone.1 | loop fusion | flops 967680 | bytes 991872 | tf_op jit(solution)/shard_map/while/body/eval_jaxpr/eq | solution.py:32
  81.7 1.5 iota_compare_fusion.9
  83.2 3.9 %fusion.73 = bf16[32,64,128]{2,1,0:T(8,128)(2,1)S(1)} fusion(bf16[160,128,1]{1,0,2:T(8,128)(2,1)S(1)} %bitcast.102, pred[189,32,160]{2,1,0:T(32,128)(4,1)} %iota_compare_fusion.8, pred[189,32,64]{2,1,0:T(32,128)(4,1)S(1)} %iota_compare_fusion.9), kind=kOutput, calls=%fused_computation.9.clone.1 | convolution fusion | flops 208338944 | bytes 1920000 | tf_op jit(solution)/shard_map/while/body/eval_jaxpr/btr,rk->btk/dot_general | solution.py:37
  87.1 2.8 %fusion.74 = f32[8,32,128]{2,1,0:T(8,128)} fusion(f32[8,32,128]{2,1,0:T(8,128)} %get-tuple-element.253, s32[]{:T(128)S(6)} %copy.92, bf16[8192,128]{1,0:T(8,128)(2,1)} %get-tuple-element.272, bf16[4,8,64,128]{3,2,1,0:T(8,128)(2,1)S(1)} %bitcast.99), kind=kOutput, calls=%fused_computation.11.clone.1 | convolution fusion | flops 67108864 | bytes 2637828 | tf_op jit(solution)/shard_map/while/body/eval_jaxpr/dot_general | solution.py:40
  94.1 2.4 %iota_compare_fusion.8 = pred[189,32,160]{2,1,0:T(32,128)(4,1)} fusion(s32[189,32]{1,0:T(8,128)S(1)} %bitcast.100), kind=kLoop, calls=%fused_computation.4.clone.1 | loop fusion | flops 967680 | bytes 991872 | tf_op jit(solution)/shard_map/while/body/eval_jaxpr/eq | solution.py:32
  96.6 1.5 iota_compare_fusion.9
  98.1 3.9 %fusion.73 = bf16[32,64,128]{2,1,0:T(8,128)(2,1)S(1)} fusion(bf16[160,128,1]{1,0,2:T(8,128)(2,1)S(1)} %bitcast.102, pred[189,32,160]{2,1,0:T(32,128)(4,1)} %iota_compare_fusion.8, pred[189,32,64]{2,1,0:T(32,128)(4,1)S(1)} %iota_compare_fusion.9), kind=kOutput, calls=%fused_computation.9.clone.1 | convolution fusion | flops 208338944 | bytes 1920000 | tf_op jit(solution)/shard_map/while/body/eval_jaxpr/btr,rk->btk/dot_general | solution.py:37
  102.0 2.8 %fusion.74 = f32[8,32,128]{2,1,0:T(8,128)} fusion(f32[8,32,128]{2,1,0:T(8,128)} %get-tuple-element.253, s32[]{:T(128)S(6)} %copy.92, bf16[8192,128]{1,0:T(8,128)(2,1)} %get-tuple-element.272, bf16[4,8,64,128]{3,2,1,0:T(8,128)(2,1)S(1)} %bitcast.99), kind=kOutput, calls=%fused_computation.11.clone.1 | convolution fusion | flops 67108864 | bytes 2637828 | tf_op jit(solution)/shard_map/while/body/eval_jaxpr/dot_general | solution.py:40
  109.0 2.4 %iota_compare_fusion.8 = pred[189,32,160]{2,1,0:T(32,128)(4,1)} fusion(s32[189,32]{1,0:T(8,128)S(1)} %bitcast.100), kind=kLoop, calls=%fused_computation.4.clone.1 | loop fusion | flops 967680 | bytes 991872 | tf_op jit(solution)/shard_map/while/body/eval_jaxpr/eq | solution.py:32
  111.5 1.5 iota_compare_fusion.9
  112.9 3.9 %fusion.73 = bf16[32,64,128]{2,1,0:T(8,128)(2,1)S(1)} fusion(bf16[160,128,1]{1,0,2:T(8,128)(2,1)S(1)} %bitcast.102, pred[189,32,160]{2,1,0:T(32,128)(4,1)} %iota_compare_fusion.8, pred[189,32,64]{2,1,0:T(32,128)(4,1)S(1)} %iota_compare_fusion.9), kind=kOutput, calls=%fused_computation.9.clone.1 | convolution fusion | flops 208338944 | bytes 1920000 | tf_op jit(solution)/shard_map/while/body/eval_jaxpr/btr,rk->btk/dot_general | solution.py:37
  116.9 2.8 %fusion.74 = f32[8,32,128]{2,1,0:T(8,128)} fusion(f32[8,32,128]{2,1,0:T(8,128)} %get-tuple-element.253, s32[]{:T(128)S(6)} %copy.92, bf16[8192,128]{1,0:T(8,128)(2,1)} %get-tuple-element.272, bf16[4,8,64,128]{3,2,1,0:T(8,128)(2,1)S(1)} %bitcast.99), kind=kOutput, calls=%fused_computation.11.clone.1 | convolution fusion | flops 67108864 | bytes 2637828 | tf_op jit(solution)/shard_map/while/body/eval_jaxpr/dot_general | solution.py:40
  123.9 2.4 %iota_compare_fusion.8 = pred[189,32,160]{2,1,0:T(32,128)(4,1)} fusion(s32[189,32]{1,0:T(8,128)S(1)} %bitcast.100), kind=kLoop, calls=%fused_computation.4.clone.1 | loop fusion | flops 967680 | bytes 991872 | tf_op jit(solution)/shard_map/while/body/eval_jaxpr/eq | solution.py:32
  126.3 1.5 iota_compare_fusion.9
  127.8 3.9 %fusion.73 = bf16[32,64,128]{2,1,0:T(8,128)(2,1)S(1)} fusion(bf16[160,128,1]{1,0,2:T(8,128)(2,1)S(1)} %bitcast.102, pred[189,32,160]{2,1,0:T(32,128)(4,1)} %iota_compare_fusion.8, pred[189,32,64]{2,1,0:T(32,128)(4,1)S(1)} %iota_compare_fusion.9), kind=kOutput, calls=%fused_computation.9.clone.1 | convolution fusion | flops 208338944 | bytes 1920000 | tf_op jit(solution)/shard_map/while/body/eval_jaxpr/btr,rk->btk/dot_general | solution.py:37
  131.8 2.8 %fusion.74 = f32[8,32,128]{2,1,0:T(8,128)} fusion(f32[8,32,128]{2,1,0:T(8,128)} %get-tuple-element.253, s32[]{:T(128)S(6)} %copy.92, bf16[8192,128]{1,0:T(8,128)(2,1)} %get-tuple-element.272, bf16[4,8,64,128]{3,2,1,0:T(8,128)(2,1)S(1)} %bitcast.99), kind=kOutput, calls=%fused_computation.11.clone.1 | convolution fusion | flops 67108864 | bytes 2637828 | tf_op jit(solution)/shard_map/while/body/eval_jaxpr/dot_general | solution.py:40
  138.7 2.4 %iota_compare_fusion.8 = pred[189,32,160]{2,1,0:T(32,128)(4,1)} fusion(s32[189,32]{1,0:T(8,128)S(1)} %bitcast.100), kind=kLoop, calls=%fused_computation.4.clone.1 | loop fusion | flops 967680 | bytes 991872 | tf_op jit(solution)/shard_map/while/body/eval_jaxpr/eq | solution.py:32
  141.2 1.5 iota_compare_fusion.9
  142.7 3.9 %fusion.73 = bf16[32,64,128]{2,1,0:T(8,128)(2,1)S(1)} fusion(bf16[160,128,1]{1,0,2:T(8,128)(2,1)S(1)} %bitcast.102, pred[189,32,160]{2,1,0:T(32,128)(4,1)} %iota_compare_fusion.8, pred[189,32,64]{2,1,0:T(32,128)(4,1)S(1)} %iota_compare_fusion.9), kind=kOutput, calls=%fused_computation.9.clone.1 | convolution fusion | flops 208338944 | bytes 1920000 | tf_op jit(solution)/shard_map/while/body/eval_jaxpr/btr,rk->btk/dot_general | solution.py:37
  146.7 2.8 %fusion.74 = f32[8,32,128]{2,1,0:T(8,128)} fusion(f32[8,32,128]{2,1,0:T(8,128)} %get-tuple-element.253, s32[]{:T(128)S(6)} %copy.92, bf16[8192,128]{1,0:T(8,128)(2,1)} %get-tuple-element.272, bf16[4,8,64,128]{3,2,1,0:T(8,128)(2,1)S(1)} %bitcast.99), kind=kOutput, calls=%fused_computation.11.clone.1 | convolution fusion | flops 67108864 | bytes 2637828 | tf_op jit(solution)/shard_map/while/body/eval_jaxpr/dot_general | solution.py:40
  153.6 2.4 %iota_compare_fusion.8 = pred[189,32,160]{2,1,0:T(32,128)(4,1)} fusion(s32[189,32]{1,0:T(8,128)S(1)} %bitcast.100), kind=kLoop, calls=%fused_computation.4.clone.1 | loop fusion | flops 967680 | bytes 991872 | tf_op jit(solution)/shard_map/while/body/eval_jaxpr/eq | solution.py:32
  156.1 1.5 iota_compare_fusion.9
  157.6 3.9 %fusion.73 = bf16[32,64,128]{2,1,0:T(8,128)(2,1)S(1)} fusion(bf16[160,128,1]{1,0,2:T(8,128)(2,1)S(1)} %bitcast.102, pred[189,32,160]{2,1,0:T(32,128)(4,1)} %iota_compare_fusion.8, pred[189,32,64]{2,1,0:T(32,128)(4,1)S(1)} %iota_compare_fusion.9), kind=kOutput, calls=%fused_computation.9.clone.1 | convolution fusion | flops 208338944 | bytes 1920000 | tf_op jit(solution)/shard_map/while/body/eval_jaxpr/btr,rk->btk/dot_general | solution.py:37
  161.5 2.8 %fusion.74 = f32[8,32,128]{2,1,0:T(8,128)} fusion(f32[8,32,128]{2,1,0:T(8,128)} %get-tuple-element.253, s32[]{:T(128)S(6)} %copy.92, bf16[8192,128]{1,0:T(8,128)(2,1)} %get-tuple-element.272, bf16[4,8,64,128]{3,2,1,0:T(8,128)(2,1)S(1)} %bitcast.99), kind=kOutput, calls=%fused_computation.11.clone.1 | convolution fusion | flops 67108864 | bytes 2637828 | tf_op jit(solution)/shard_map/while/body/eval_jaxpr/dot_general | solution.py:40
  168.5 2.4 %iota_compare_fusion.8 = pred[189,32,160]{2,1,0:T(32,128)(4,1)} fusion(s32[189,32]{1,0:T(8,128)S(1)} %bitcast.100), kind=kLoop, calls=%fused_computation.4.clone.1 | loop fusion | flops 967680 | bytes 991872 | tf_op jit(solution)/shard_map/while/body/eval_jaxpr/eq | solution.py:32
  171.0 1.5 iota_compare_fusion.9
  172.5 3.9 %fusion.73 = bf16[32,64,128]{2,1,0:T(8,128)(2,1)S(1)} fusion(bf16[160,128,1]{1,0,2:T(8,128)(2,1)S(1)} %bitcast.102, pred[189,32,160]{2,1,0:T(32,128)(4,1)} %iota_compare_fusion.8, pred[189,32,64]{2,1,0:T(32,128)(4,1)S(1)} %iota_compare_fusion.9), kind=kOutput, calls=%fused_computation.9.clone.1 | convolution fusion | flops 208338944 | bytes 1920000 | tf_op jit(solution)/shard_map/while/body/eval_jaxpr/btr,rk->btk/dot_general | solution.py:37
  176.4 2.8 %fusion.74 = f32[8,32,128]{2,1,0:T(8,128)} fusion(f32[8,32,128]{2,1,0:T(8,128)} %get-tuple-element.253, s32[]{:T(128)S(6)} %copy.92, bf16[8192,128]{1,0:T(8,128)(2,1)} %get-tuple-element.272, bf16[4,8,64,128]{3,2,1,0:T(8,128)(2,1)S(1)} %bitcast.99), kind=kOutput, calls=%fused_computation.11.clone.1 | convolution fusion | flops 67108864 | bytes 2637828 | tf_op jit(solution)/shard_map/while/body/eval_jaxpr/dot_general | solution.py:40
  180.3 4.9 %all_gather.11 = bf16[512,128]{1,0:T(8,128)(2,1)S(1)} all-gather(bf16[256,128]{1,0:T(8,128)(2,1)S(1)} %fusion.52), channel_id=1, replica_groups=mesh['space'=16,'batch'=2] {'batch'}, dimensions={0}, use_global_device_ids=true | all-gather | bytes 196608 | tf_op jit(solution)/shard_map/all_gather | solution.py:117
  185.2 1.2 fusion.49
  (148 shorter events, 23.4 us)
Async XLA Ops:
  6.5 178.7 %copy-start = (bf16[512,16,128]{2,1,0:T(8,128)(2,1)S(1)}, bf16[512,16,128]{2,1,0:T(8,128)(2,1)}, u32[]{:S(2)}) copy-start(bf16[512,16,128]{2,1,0:T(8,128)(2,1)} %param.22) | copy-start | bytes 6291460
  6.5 15.7 %reduce-scatter.3.cloned.1.call-start = ((), (), s32[]{:S(2)}) async-start(), calls=%async_computation.2 | async-start | bytes 24576 | tf_op jit(solution)/shard_map/reduce_scatter | solution.py:89
  7.3 35.9 %reduce-scatter.5.cloned.1.call-start = ((), (), s32[]{:S(2)}) async-start(), calls=%async_computation.3 | async-start | bytes 196608 | tf_op jit(solution)/shard_map/reduce_scatter | solution.py:86
  22.2 6.0 %collective-permute-start = (bf16[32,128]{1,0:T(8,128)(2,1)}, bf16[32,128]{1,0:T(8,128)(2,1)S(1)}, u32[]{:S(2)}, u32[]{:S(2)}) collective-permute-start(bf16[32,128]{1,0:T(8,128)(2,1)} %reduce-scatter.3.cloned.1.call-done), channel_id=1, source_target_pairs={{0,2},{2,0},{4,6},{6,4},{8,10},{10,8},{12,14},{14,12},{16,18},{18,... | collective-permute-start | bytes 24584 | tf_op jit(solution)/shard_map/ppermute | solution.py:13
  22.9 5.4 %collective-permute-start.1 = (bf16[32,128]{1,0:T(8,128)(2,1)}, bf16[32,128]{1,0:T(8,128)(2,1)S(1)}, u32[]{:S(2)}, u32[]{:S(2)}) collective-permute-start(bf16[32,128]{1,0:T(8,128)(2,1)} %reduce-scatter.3.cloned.1.call-done), channel_id=1, source_target_pairs={{0,4},{2,6},{4,0},{6,2},{8,12},{10,14},{12,8},{14,10},{16,20},{18,... | collective-permute-start | bytes 24584 | tf_op jit(solution)/shard_map/ppermute | solution.py:13
  24.4 3.9 %collective-permute-start.2 = (bf16[32,128]{1,0:T(8,128)(2,1)}, bf16[32,128]{1,0:T(8,128)(2,1)S(1)}, u32[]{:S(2)}, u32[]{:S(2)}) collective-permute-start(bf16[32,128]{1,0:T(8,128)(2,1)} %reduce-scatter.3.cloned.1.call-done), channel_id=1, source_target_pairs={{0,8},{2,10},{4,12},{6,14},{8,0},{10,2},{12,4},{14,6},{16,24},{18,... | collective-permute-start | bytes 24584 | tf_op jit(solution)/shard_map/ppermute | solution.py:13
  25.9 4.8 %collective-permute-start.3 = (bf16[32,128]{1,0:T(8,128)(2,1)}, bf16[32,128]{1,0:T(8,128)(2,1)S(1)}, u32[]{:S(2)}, u32[]{:S(2)}) collective-permute-start(bf16[32,128]{1,0:T(8,128)(2,1)} %reduce-scatter.3.cloned.1.call-done), channel_id=1, source_target_pairs={{0,16},{2,18},{4,20},{6,22},{8,24},{10,26},{12,28},{14,30},{16,0},... | collective-permute-start | bytes 24584 | tf_op jit(solution)/shard_map/ppermute | solution.py:13
  35.4 4.7 %copy-start.5 = (f32[64,128]{1,0:T(8,128)S(1)}, f32[64,128]{1,0:T(8,128)}, u32[]{:S(2)}) copy-start(f32[64,128]{1,0:T(8,128)} %param.15) | copy-start | bytes 98308
  43.2 4.8 %collective-permute-start.4 = (bf16[256,128]{1,0:T(8,128)(2,1)}, bf16[256,128]{1,0:T(8,128)(2,1)S(1)}, u32[]{:S(2)}, u32[]{:S(2)}) collective-permute-start(bf16[256,128]{1,0:T(8,128)(2,1)} %reduce-scatter.5.cloned.1.call-done), channel_id=1, source_target_pairs={{0,2},{2,0},{4,6},{6,4},{8,10},{10,8},{12,14},{14,12},{16,18},{18,... | collective-permute-start | bytes 196616 | tf_op jit(solution)/shard_map/ppermute | solution.py:13
  44.0 4.7 %collective-permute-start.5 = (bf16[256,128]{1,0:T(8,128)(2,1)}, bf16[256,128]{1,0:T(8,128)(2,1)S(1)}, u32[]{:S(2)}, u32[]{:S(2)}) collective-permute-start(bf16[256,128]{1,0:T(8,128)(2,1)} %reduce-scatter.5.cloned.1.call-done), channel_id=1, source_target_pairs={{0,4},{2,6},{4,0},{6,2},{8,12},{10,14},{12,8},{14,10},{16,20},{18,... | collective-permute-start | bytes 196616 | tf_op jit(solution)/shard_map/ppermute | solution.py:13
  44.6 4.5 %collective-permute-start.6 = (bf16[256,128]{1,0:T(8,128)(2,1)}, bf16[256,128]{1,0:T(8,128)(2,1)S(1)}, u32[]{:S(2)}, u32[]{:S(2)}) collective-permute-start(bf16[256,128]{1,0:T(8,128)(2,1)} %reduce-scatter.5.cloned.1.call-done), channel_id=1, source_target_pairs={{0,8},{2,10},{4,12},{6,14},{8,0},{10,2},{12,4},{14,6},{16,24},{18,... | collective-permute-start | bytes 196616 | tf_op jit(solution)/shard_map/ppermute | solution.py:13
  45.6 6.0 %collective-permute-start.7 = (bf16[256,128]{1,0:T(8,128)(2,1)}, bf16[256,128]{1,0:T(8,128)(2,1)S(1)}, u32[]{:S(2)}, u32[]{:S(2)}) collective-permute-start(bf16[256,128]{1,0:T(8,128)(2,1)} %reduce-scatter.5.cloned.1.call-done), channel_id=1, source_target_pairs={{0,16},{2,18},{4,20},{6,22},{8,24},{10,26},{12,28},{14,30},{16,0},... | collective-permute-start | bytes 196616 | tf_op jit(solution)/shard_map/ppermute | solution.py:13
  60.2 6.6 %copy-start.1 = (s32[8,189,32]{1,2,0:T(8,128)}, s32[8,189,32]{1,2,0:T(8,128)S(1)}, u32[]{:S(2)}) copy-start(s32[8,189,32]{1,2,0:T(8,128)S(1)} %get-tuple-element.268) | copy-start | bytes 580612 | tf_op jit(solution)/shard_map/while
  60.2 6.6 %copy-start.3 = (s32[8,189,32]{1,2,0:T(8,128)}, s32[8,189,32]{1,2,0:T(8,128)S(1)}, u32[]{:S(2)}) copy-start(s32[8,189,32]{1,2,0:T(8,128)S(1)} %get-tuple-element.269) | copy-start | bytes 580612 | tf_op jit(solution)/shard_map/while
  72.2 2.8 %copy-start.2 = (s32[8,189,32]{1,2,0:T(8,128)S(1)}, s32[8,189,32]{1,2,0:T(8,128)}, u32[]{:S(2)}) copy-start(s32[8,189,32]{1,2,0:T(8,128)} %copy-done.1) | copy-start | bytes 580612 | tf_op jit(solution)/shard_map/while
  72.2 2.8 %copy-start.4 = (s32[8,189,32]{1,2,0:T(8,128)S(1)}, s32[8,189,32]{1,2,0:T(8,128)}, u32[]{:S(2)}) copy-start(s32[8,189,32]{1,2,0:T(8,128)} %copy-done.3) | copy-start | bytes 580612 | tf_op jit(solution)/shard_map/while
  75.1 6.6 %copy-start.1 = (s32[8,189,32]{1,2,0:T(8,128)}, s32[8,189,32]{1,2,0:T(8,128)S(1)}, u32[]{:S(2)}) copy-start(s32[8,189,32]{1,2,0:T(8,128)S(1)} %get-tuple-element.268) | copy-start | bytes 580612 | tf_op jit(solution)/shard_map/while
  75.1 6.6 %copy-start.3 = (s32[8,189,32]{1,2,0:T(8,128)}, s32[8,189,32]{1,2,0:T(8,128)S(1)}, u32[]{:S(2)}) copy-start(s32[8,189,32]{1,2,0:T(8,128)S(1)} %get-tuple-element.269) | copy-start | bytes 580612 | tf_op jit(solution)/shard_map/while
  87.1 2.8 %copy-start.2 = (s32[8,189,32]{1,2,0:T(8,128)S(1)}, s32[8,189,32]{1,2,0:T(8,128)}, u32[]{:S(2)}) copy-start(s32[8,189,32]{1,2,0:T(8,128)} %copy-done.1) | copy-start | bytes 580612 | tf_op jit(solution)/shard_map/while
  87.1 2.8 %copy-start.4 = (s32[8,189,32]{1,2,0:T(8,128)S(1)}, s32[8,189,32]{1,2,0:T(8,128)}, u32[]{:S(2)}) copy-start(s32[8,189,32]{1,2,0:T(8,128)} %copy-done.3) | copy-start | bytes 580612 | tf_op jit(solution)/shard_map/while
  89.9 6.6 %copy-start.1 = (s32[8,189,32]{1,2,0:T(8,128)}, s32[8,189,32]{1,2,0:T(8,128)S(1)}, u32[]{:S(2)}) copy-start(s32[8,189,32]{1,2,0:T(8,128)S(1)} %get-tuple-element.268) | copy-start | bytes 580612 | tf_op jit(solution)/shard_map/while
  89.9 6.6 %copy-start.3 = (s32[8,189,32]{1,2,0:T(8,128)}, s32[8,189,32]{1,2,0:T(8,128)S(1)}, u32[]{:S(2)}) copy-start(s32[8,189,32]{1,2,0:T(8,128)S(1)} %get-tuple-element.269) | copy-start | bytes 580612 | tf_op jit(solution)/shard_map/while
  102.0 2.8 %copy-start.2 = (s32[8,189,32]{1,2,0:T(8,128)S(1)}, s32[8,189,32]{1,2,0:T(8,128)}, u32[]{:S(2)}) copy-start(s32[8,189,32]{1,2,0:T(8,128)} %copy-done.1) | copy-start | bytes 580612 | tf_op jit(solution)/shard_map/while
  102.0 2.8 %copy-start.4 = (s32[8,189,32]{1,2,0:T(8,128)S(1)}, s32[8,189,32]{1,2,0:T(8,128)}, u32[]{:S(2)}) copy-start(s32[8,189,32]{1,2,0:T(8,128)} %copy-done.3) | copy-start | bytes 580612 | tf_op jit(solution)/shard_map/while
  104.8 6.6 %copy-start.1 = (s32[8,189,32]{1,2,0:T(8,128)}, s32[8,189,32]{1,2,0:T(8,128)S(1)}, u32[]{:S(2)}) copy-start(s32[8,189,32]{1,2,0:T(8,128)S(1)} %get-tuple-element.268) | copy-start | bytes 580612 | tf_op jit(solution)/shard_map/while
  104.8 6.6 %copy-start.3 = (s32[8,189,32]{1,2,0:T(8,128)}, s32[8,189,32]{1,2,0:T(8,128)S(1)}, u32[]{:S(2)}) copy-start(s32[8,189,32]{1,2,0:T(8,128)S(1)} %get-tuple-element.269) | copy-start | bytes 580612 | tf_op jit(solution)/shard_map/while
  116.9 2.8 %copy-start.2 = (s32[8,189,32]{1,2,0:T(8,128)S(1)}, s32[8,189,32]{1,2,0:T(8,128)}, u32[]{:S(2)}) copy-start(s32[8,189,32]{1,2,0:T(8,128)} %copy-done.1) | copy-start | bytes 580612 | tf_op jit(solution)/shard_map/while
  116.9 2.8 %copy-start.4 = (s32[8,189,32]{1,2,0:T(8,128)S(1)}, s32[8,189,32]{1,2,0:T(8,128)}, u32[]{:S(2)}) copy-start(s32[8,189,32]{1,2,0:T(8,128)} %copy-done.3) | copy-start | bytes 580612 | tf_op jit(solution)/shard_map/while
  119.7 6.6 %copy-start.1 = (s32[8,189,32]{1,2,0:T(8,128)}, s32[8,189,32]{1,2,0:T(8,128)S(1)}, u32[]{:S(2)}) copy-start(s32[8,189,32]{1,2,0:T(8,128)S(1)} %get-tuple-element.268) | copy-start | bytes 580612 | tf_op jit(solution)/shard_map/while
  119.7 6.6 %copy-start.3 = (s32[8,189,32]{1,2,0:T(8,128)}, s32[8,189,32]{1,2,0:T(8,128)S(1)}, u32[]{:S(2)}) copy-start(s32[8,189,32]{1,2,0:T(8,128)S(1)} %get-tuple-element.269) | copy-start | bytes 580612 | tf_op jit(solution)/shard_map/while
  131.8 2.8 %copy-start.2 = (s32[8,189,32]{1,2,0:T(8,128)S(1)}, s32[8,189,32]{1,2,0:T(8,128)}, u32[]{:S(2)}) copy-start(s32[8,189,32]{1,2,0:T(8,128)} %copy-done.1) | copy-start | bytes 580612 | tf_op jit(solution)/shard_map/while
  131.8 2.8 %copy-start.4 = (s32[8,189,32]{1,2,0:T(8,128)S(1)}, s32[8,189,32]{1,2,0:T(8,128)}, u32[]{:S(2)}) copy-start(s32[8,189,32]{1,2,0:T(8,128)} %copy-done.3) | copy-start | bytes 580612 | tf_op jit(solution)/shard_map/while
  134.6 6.6 %copy-start.1 = (s32[8,189,32]{1,2,0:T(8,128)}, s32[8,189,32]{1,2,0:T(8,128)S(1)}, u32[]{:S(2)}) copy-start(s32[8,189,32]{1,2,0:T(8,128)S(1)} %get-tuple-element.268) | copy-start | bytes 580612 | tf_op jit(solution)/shard_map/while
  134.6 6.6 %copy-start.3 = (s32[8,189,32]{1,2,0:T(8,128)}, s32[8,189,32]{1,2,0:T(8,128)S(1)}, u32[]{:S(2)}) copy-start(s32[8,189,32]{1,2,0:T(8,128)S(1)} %get-tuple-element.269) | copy-start | bytes 580612 | tf_op jit(solution)/shard_map/while
  146.6 2.8 %copy-start.2 = (s32[8,189,32]{1,2,0:T(8,128)S(1)}, s32[8,189,32]{1,2,0:T(8,128)}, u32[]{:S(2)}) copy-start(s32[8,189,32]{1,2,0:T(8,128)} %copy-done.1) | copy-start | bytes 580612 | tf_op jit(solution)/shard_map/while
  146.6 2.8 %copy-start.4 = (s32[8,189,32]{1,2,0:T(8,128)S(1)}, s32[8,189,32]{1,2,0:T(8,128)}, u32[]{:S(2)}) copy-start(s32[8,189,32]{1,2,0:T(8,128)} %copy-done.3) | copy-start | bytes 580612 | tf_op jit(solution)/shard_map/while
  149.5 6.6 %copy-start.1 = (s32[8,189,32]{1,2,0:T(8,128)}, s32[8,189,32]{1,2,0:T(8,128)S(1)}, u32[]{:S(2)}) copy-start(s32[8,189,32]{1,2,0:T(8,128)S(1)} %get-tuple-element.268) | copy-start | bytes 580612 | tf_op jit(solution)/shard_map/while
  149.5 6.6 %copy-start.3 = (s32[8,189,32]{1,2,0:T(8,128)}, s32[8,189,32]{1,2,0:T(8,128)S(1)}, u32[]{:S(2)}) copy-start(s32[8,189,32]{1,2,0:T(8,128)S(1)} %get-tuple-element.269) | copy-start | bytes 580612 | tf_op jit(solution)/shard_map/while
  161.5 2.8 %copy-start.2 = (s32[8,189,32]{1,2,0:T(8,128)S(1)}, s32[8,189,32]{1,2,0:T(8,128)}, u32[]{:S(2)}) copy-start(s32[8,189,32]{1,2,0:T(8,128)} %copy-done.1) | copy-start | bytes 580612 | tf_op jit(solution)/shard_map/while
  161.5 2.8 %copy-start.4 = (s32[8,189,32]{1,2,0:T(8,128)S(1)}, s32[8,189,32]{1,2,0:T(8,128)}, u32[]{:S(2)}) copy-start(s32[8,189,32]{1,2,0:T(8,128)} %copy-done.3) | copy-start | bytes 580612 | tf_op jit(solution)/shard_map/while
  164.3 6.6 %copy-start.1 = (s32[8,189,32]{1,2,0:T(8,128)}, s32[8,189,32]{1,2,0:T(8,128)S(1)}, u32[]{:S(2)}) copy-start(s32[8,189,32]{1,2,0:T(8,128)S(1)} %get-tuple-element.268) | copy-start | bytes 580612 | tf_op jit(solution)/shard_map/while
  164.3 6.6 %copy-start.3 = (s32[8,189,32]{1,2,0:T(8,128)}, s32[8,189,32]{1,2,0:T(8,128)S(1)}, u32[]{:S(2)}) copy-start(s32[8,189,32]{1,2,0:T(8,128)S(1)} %get-tuple-element.269) | copy-start | bytes 580612 | tf_op jit(solution)/shard_map/while
  176.4 2.8 %copy-start.2 = (s32[8,189,32]{1,2,0:T(8,128)S(1)}, s32[8,189,32]{1,2,0:T(8,128)}, u32[]{:S(2)}) copy-start(s32[8,189,32]{1,2,0:T(8,128)} %copy-done.1) | copy-start | bytes 580612 | tf_op jit(solution)/shard_map/while
  176.4 2.8 %copy-start.4 = (s32[8,189,32]{1,2,0:T(8,128)S(1)}, s32[8,189,32]{1,2,0:T(8,128)}, u32[]{:S(2)}) copy-start(s32[8,189,32]{1,2,0:T(8,128)} %copy-done.3) | copy-start | bytes 580612 | tf_op jit(solution)/shard_map/while
  179.2 7.3 %copy-start.6 = (s32[1,512]{1,0:T(1,128)S(1)}, s32[1,512]{1,0:T(1,128)}, u32[]{:S(2)}) copy-start(s32[1,512]{1,0:T(1,128)} %param.23) | copy-start | bytes 6148
Sparse Core Ops, SparseCore 0:
  9.5 12.6 reduce-scatter.2
  24.4 10.7 reduce-scatter.4
where the time goes:
time: 196 us; the launch traced here: 194 us
  matrix products  62.8 us (32%)
  other arithmetic  36.3 us (19%)
  loops' own time  21 us (11%)
  blocking collectives  18.2 us (9%)
  local copies, waits for them, and re-layouts  17.6 us (9%)
  waiting for transfers between devices  15.3 us (8%)
  between operations  13.5 us (7%)
  starting transfers between devices  9.37 us (5%)
    dot_general x9, matrix products, one_piece(): jnp.einsum('btr,rk->btk', counted, nearby, preferred_element_type=jnp.flo...  36.1 us
    dot_general x8, matrix products, one_piece(): jnp.dot(grouped.reshape(piece_rows, kind_count * coef_width), flat_ops, p...  22.4 us
    eq x9, other arithmetic, one_piece(): chosen = (sources[:, :, None] == column_iota).astype(jnp.bfloat16)  21.3 us
    another operation x1, loops' own time, far_field(): lax.map(one_piece, (source_pieces, kind_pieces, starts))  21 us
    eq x9, other arithmetic, one_piece(): onehot = (kinds[:, :, None] == kinds_iota).astype(jnp.bfloat16)  13.2 us
    ppermute x8, starting transfers between devices, partner(): lax.ppermute(shard, axis, [(i, i ^ 1 << apart) for i in range(lax.axis_si...  9.33 us
    all_gather x1, blocking collectives, body(): lax.all_gather(fine_pieces, 'batch', axis=1, tiled=True)  8.59 us
    reduce_scatter x1, waiting for transfers between devices, body(): lax.psum_scatter(parent_terms.astype(jnp.bfloat16), 'batch', scatter_dime...  8 us
  transfers between devices with their start and end apart: 10, of which 5 were waited for; matrix products, arithmetic and copies ran while one was open for 8% of the time, Pallas kernels for 0%

commit v1 on v0

v1 whole, which is shorter than its diff:
```python
import functools

import jax
import jax.numpy as jnp
from jax import lax
from jax.experimental import pallas as pl
from jax.experimental.pallas import tpu as pltpu
from jax.sharding import PartitionSpec as P

NTERMS = 121
WINDOW = 32
LANES = 128
VMEM = pl.BlockSpec(memory_space=pltpu.VMEM)
SMEM = pl.BlockSpec(memory_space=pltpu.SMEM)


def round_up(value, step):
    return -(-value // step) * step


def rotate(value, axis, step):
    size = lax.axis_size(axis)
    return lax.ppermute(value, axis, [(i, (i + step) % size) for i in range(size)])


def partner(value, axis, apart):
    return lax.ppermute(value, axis, [(i, i ^ 1 << apart) for i in range(lax.axis_size(axis))])


def count_kernel(
    widths, kinds, columns, member_ref, fs_ref, fo_ref, ps_ref, po_ref, out_ref, *scratch
):
    member = member_ref[0]
    depth = scratch[0].shape[1]
    half = jnp.bfloat16
    rows_iota = lax.broadcasted_iota(jnp.int32, (16, depth), 0).astype(half)
    one = jnp.ones((), half)
    zero = jnp.zeros((), half)

    def hot(row_ref, row, size):
        values = jnp.broadcast_to(row_ref[pl.ds(row, 1), :], (16, depth)).astype(half)
        pieces = [jnp.where(values == rows_iota + 16 * k, one, zero) for k in range(size // 16)]
        return jnp.concatenate(pieces, 0).astype(jnp.float8_e4m3fn)

    done = 0
    for (source_ref, kind_ref), (source_rows, kind_rows), width in zip(
        ((fs_ref, fo_ref), (ps_ref, po_ref)), (scratch[:2], scratch[2:]), widths
    ):
        length, total = source_ref.shape
        whole = length // 8 * 8
        span = width if width % LANES == 0 else total
        offset = 0 if span == width else member * width
        for ref, rows in ((source_ref, source_rows), (kind_ref, kind_rows)):
            if span == total:
                body, tail = ref[:whole, :], ref[whole:, :]
            else:
                lanes = pl.ds(pl.multiple_of(member * width, LANES), width)
                body, tail = ref[:whole, lanes], ref[whole:, lanes]
            pad = jnp.full((depth - length, span), -1, jnp.int32)
            entries = jnp.concatenate([body, tail, pad], 0).astype(jnp.float32)
            extra = rows.shape[0] - span
            if extra:
                entries = jnp.concatenate([entries, jnp.zeros((depth, extra), jnp.float32)], 1)
            rows[...] = entries.T

        def one_box(box, _, offset=offset, done=done, source_rows=source_rows, kind_rows=kind_rows):
            source_hot = hot(source_rows, box + offset, columns)
            kind_hot = hot(kind_rows, box + offset, kinds)
            counted = lax.dot_general(
                kind_hot, source_hot, (((1,), (1,)), ((), ())), preferred_element_type=jnp.float32
            )
            start = pl.multiple_of((box + done) * kinds, kinds)
            out_ref[pl.ds(start, kinds), :] = counted.astype(half)
            return 0

        lax.fori_loop(0, width, one_box, 0, unroll=8)
        done += width


def count_entries(member, fine_source, fine_kind, parent_source, parent_kind, widths, kinds, columns):
    length = fine_source.shape[0]
    depth = round_up(length, LANES)
    boxes = sum(widths)
    scratch = []
    for source, width in ((fine_source, widths[0]), (parent_source, widths[1])):
        span = width if width % LANES == 0 else source.shape[1]
        scratch += [pltpu.VMEM((round_up(span, LANES), depth), jnp.float32)] * 2
    return pl.pallas_call(
        functools.partial(count_kernel, widths, kinds, columns),
        out_shape=jax.ShapeDtypeStruct((boxes * kinds, columns), jnp.bfloat16),
        in_specs=[SMEM] + [VMEM] * 4,
        out_specs=VMEM,
        scratch_shapes=scratch,
        compiler_params=pltpu.CompilerParams(vmem_limit_bytes=24 << 20),
        cost_estimate=pl.CostEstimate(
            flops=2 * boxes * depth * kinds * columns * 4,
            bytes_accessed=boxes * kinds * columns * 2,
            transcendentals=0,
        ),
        name="counts",
    )(member, fine_source, fine_kind, parent_source, parent_kind)


def local_kernel(
    widths, kinds, member_ref, count_ref, *refs
):
    (b0, b1, b2, b3, b4, ops_ref, coarse_ref, shift_ref, out_ref, grouped, total, moved) = refs
    blocks = (b0, b1, b2, b3, b4)
    member = member_ref[0]
    fine, parent = widths
    coef = out_ref.shape[1]
    rows = WINDOW * kinds

    def one_window(window, _):
        start = pl.multiple_of(window * WINDOW, WINDOW)
        nearby = jnp.concatenate([ref[pl.ds(start, WINDOW), :] for ref in blocks], 0)
        at = pl.multiple_of(window * rows, rows)
        grouped[pl.ds(at, rows), :] = jnp.dot(
            count_ref[pl.ds(at, rows), :], nearby, preferred_element_type=jnp.float32
        )
        return 0

    lax.fori_loop(0, fine // WINDOW, one_window, 0)
    spread = max(parent, WINDOW)
    for piece in range(spread // WINDOW):
        start = fine + piece * WINDOW
        nearby = jnp.concatenate([ref[start : start + WINDOW, :] for ref in blocks], 0)
        count = min(parent, WINDOW) * kinds
        at = (fine + piece * WINDOW) * kinds
        grouped[at : at + count, :] = jnp.dot(
            count_ref[at : at + count, :], nearby, preferred_element_type=jnp.float32
        )

    boxes = fine + parent
    step = 8
    total[...] = jnp.zeros_like(total)

    def some_kinds(at, _):
        picked = [
            grouped[pl.ds(at * step + k, boxes, stride=kinds), :].astype(jnp.bfloat16)
            for k in range(step)
        ]
        start = pl.multiple_of(at * step * coef, step * coef)
        total[...] += jnp.dot(
            jnp.concatenate(picked, 1),
            ops_ref[pl.ds(start, step * coef), :],
            preferred_element_type=jnp.float32,
        )
        return 0

    lax.fori_loop(0, kinds // step, some_kinds, 0)
    begin = member * parent
    if parent % 8 == 0:
        begin = pl.multiple_of(begin, 8)
    parent_local = coarse_ref[pl.ds(begin, parent), :] + total[fine:, :]
    parent_local = parent_local.astype(jnp.bfloat16)
    octants = shift_ref.shape[0]
    for octant in range(octants):
        moved[pl.ds(octant, parent, stride=octants), :] = jnp.dot(
            parent_local, shift_ref[octant], preferred_element_type=jnp.float32
        )
    whole = moved[...] + total[:fine, :]
    keep = lax.broadcasted_iota(jnp.int32, whole.shape, 1) < NTERMS
    out_ref[...] = jnp.where(keep, whole, 0.0).astype(jnp.bfloat16)


def local_of(member, counted, blocks, flat_ops, coarse, child_shift, widths, kinds):
    fine, parent = widths
    coef = flat_ops.shape[1]
    boxes = fine + parent
    return pl.pallas_call(
        functools.partial(local_kernel, widths, kinds),
        out_shape=jax.ShapeDtypeStruct((fine, coef), jnp.bfloat16),
        in_specs=[SMEM] + [VMEM] * 9,
        out_specs=VMEM,
        scratch_shapes=[
            pltpu.VMEM((boxes * kinds, coef), jnp.float32),
            pltpu.VMEM((boxes, coef), jnp.float32),
            pltpu.VMEM((fine, coef), jnp.float32),
        ],
        compiler_params=pltpu.CompilerParams(vmem_limit_bytes=32 << 20),
        cost_estimate=pl.CostEstimate(
            flops=8 * boxes * kinds * coef * 256,
            bytes_accessed=boxes * kinds * coef * 4,
            transcendentals=0,
        ),
        name="far",
    )(member, counted, *blocks, flat_ops, coarse, child_shift)


def slots_of(basis_ref, counts_ref, box, local):
    count, coef = local.shape
    slots = basis_ref.shape[1]
    pairs = count // 2
    odd = lax.broadcasted_iota(jnp.int32, local.shape, 0) % 2
    zero = jnp.zeros_like(local)
    right = jnp.concatenate(
        [jnp.where(odd == 0, local, zero), jnp.where(odd == 1, local, zero)], 1
    )
    left = basis_ref[pl.ds(box, count)].reshape(pairs, 2, slots, coef)
    left = jnp.concatenate([left[:, 0], left[:, 1]], 2).reshape(pairs * slots, 2 * coef)
    values = lax.dot_general(
        left, right, (((1,), (1,)), ((), ())), preferred_element_type=jnp.float32
    ).reshape(pairs, slots, count)
    lane = lax.broadcasted_iota(jnp.int32, (slots, count), 1) // 2
    summed = jnp.zeros((slots, count), jnp.float32)
    for pair in range(pairs):
        summed += jnp.where(lane == pair, values[pair], 0.0)
    slot = lax.broadcasted_iota(jnp.int32, summed.shape, 0)
    limit = counts_ref[:, pl.ds(box, count)]
    return jnp.where(slot < limit, summed, 0.0)


def own_kernel(member_ref, local_ref, basis_ref, counts_ref, out_ref):
    width = local_ref.shape[0]
    for piece in range(width // LANES):
        box = pl.multiple_of(member_ref[0] * width + piece * LANES, LANES)
        at = slice(piece * LANES, (piece + 1) * LANES)
        out_ref[:, at] = slots_of(basis_ref, counts_ref, box, local_ref[at, :])


def other_kernel(member_ref, local_ref, basis_ref, counts_ref, own_ref, out_ref):
    width = local_ref.shape[0]
    out_ref[:, pl.ds(pl.multiple_of(member_ref[0] * width, LANES), width)] = own_ref[...]
    for piece in range(width // LANES):
        box = pl.multiple_of((1 - member_ref[0]) * width + piece * LANES, LANES)
        at = slice(piece * LANES, (piece + 1) * LANES)
        out_ref[:, pl.ds(box, LANES)] = slots_of(basis_ref, counts_ref, box, local_ref[at, :])


def evaluate(kernel, columns, member, local, basis, counts, *more):
    slots = basis.shape[1]
    return pl.pallas_call(
        kernel,
        out_shape=jax.ShapeDtypeStruct((slots, columns), jnp.float32),
        in_specs=[SMEM] + [VMEM] * (3 + len(more)),
        out_specs=VMEM,
        compiler_params=pltpu.CompilerParams(vmem_limit_bytes=16 << 20),
        cost_estimate=pl.CostEstimate(
            flops=2 * local.shape[0] * slots * 256 * 128,
            bytes_accessed=local.shape[0] * slots * 256,
            transcendentals=0,
        ),
        name="slots",
    )(member, local, basis, counts, *more)


def body(
    fine_parts,
    parent_parts,
    coarse_local,
    fine_source,
    fine_operator,
    parent_source,
    parent_operator,
    operators,
    child_shift,
    basis,
    counts,
):
    group = lax.axis_size("batch")
    member = lax.axis_index("batch")
    kinds, coef, _ = operators.shape
    fine_total, parent_total = fine_source.shape[1], parent_source.shape[1]
    widths = (fine_total // group, parent_total // group)
    index = member.astype(jnp.int32).reshape(1)

    def share(whose):
        fine_size, parent_size = max(widths[0], WINDOW), max(widths[1], WINDOW)
        fine_at = whose * widths[0] // WINDOW * WINDOW
        parent_at = whose * widths[1] // WINDOW * WINDOW
        return jnp.concatenate(
            [
                lax.dynamic_slice_in_dim(fine_parts[0], fine_at, fine_size, 0),
                lax.dynamic_slice_in_dim(parent_parts[0], parent_at, parent_size, 0),
            ],
            0,
        )

    summed = share(member).astype(jnp.float32)
    for step in range(1, group):
        summed += rotate(share((member + step) % group), "batch", step).astype(jnp.float32)
    own = summed.astype(jnp.bfloat16)
    blocks = [own] + [partner(own, "space", bit) for bit in range(4)]
    counted = count_entries(
        index,
        fine_source,
        fine_operator,
        parent_source,
        parent_operator,
        widths,
        kinds,
        5 * WINDOW,
    )
    local = local_of(
        index,
        counted,
        blocks,
        operators.reshape(kinds * coef, coef),
        coarse_local,
        child_shift,
        widths,
        kinds,
    )
    if group == 2 and widths[0] % LANES == 0:
        other = rotate(local, "batch", 1)
        mine = evaluate(own_kernel, widths[0], index, local, basis, counts)
        return evaluate(other_kernel, fine_total, index, other, basis, counts, mine)
    gathered = jnp.zeros((fine_total, coef), local.dtype)
    for step in range(group):
        piece = rotate(local, "batch", step) if step else local
        at = (member - step) % group * widths[0]
        gathered = lax.dynamic_update_slice_in_dim(gathered, piece, at, 0)
    return evaluate(own_kernel, fine_total, index * 0, gathered, basis, counts)


def solution(mesh):
    placed = (
        P("batch", "space", None),
        P("batch", "space", None),
        P("space", None),
        P(None, "space"),
        P(None, "space"),
        P(None, "space"),
        P(None, "space"),
        P(),
        P(),
        P("space", "batch", None),
        P("batch", "space"),
    )
    return jax.shard_map(
        body, mesh=mesh, in_specs=placed, out_specs=P("batch", "space"), check_vma=False
    )
```

time: 196 us -> 39.2 us (0.20)
  matrix products: 62.8 us -> 0 us
  other arithmetic: 36.3 us -> 0.03 us
  loops' own time: 21 us -> 0 us
  Pallas kernels: 0 us -> 19.5 us
  blocking collectives: 18.2 us -> 0 us
  between operations: 13.5 us -> 0.13 us
  waiting for transfers between devices: 15.3 us -> 2.79 us
  local copies, waits for them, and re-layouts: 17.6 us -> 5.48 us
    dot_general x19 -> x0, matrix products: 62.8 us -> none  [the longest x9 36.1 us: one_piece(): jnp.einsum('btr,rk->btk', counted, nearby, preferred_element_type=jnp.flo...]
    eq x18 -> x0, other arithmetic: 34.5 us -> none  [the longest x9 21.3 us: one_piece(): chosen = (sources[:, :, None] == column_iota).astype(jnp.bfloat16)]
    another operation x1 -> x0, loops' own time: 21 us -> none  [far_field(): lax.map(one_piece, (source_pieces, kind_pieces, starts))]
    pallas_call x0 -> x4, Pallas kernels: none -> 19.5 us  [the longest x1 10.1 us: local_of(): pl.pallas_call(functools.partial(local_kernel, widths, kinds), out_shape=...]
    all_gather x3 -> x0, blocking collectives: 18.2 us -> none  [the longest x1 8.59 us: body(): lax.all_gather(fine_pieces, 'batch', axis=1, tiled=True)]
    dynamic_slice x45 -> x2, local copies, waits for them, and re-layouts: 15.5 us -> 1.6 us  [the longest x1 0.88 us: share(): lax.dynamic_slice_in_dim(fine_parts[0], fine_at, fine_size, 0)]
    reduce_scatter x2 -> x0, waiting for transfers between devices: 8 us -> none  [the longest x1 8 us: body(): lax.psum_scatter(parent_terms.astype(jnp.bfloat16), 'batch', scatter_dime...]
    ppermute x8 -> x6, waiting for transfers between devices: 5.92 us -> 2.79 us  [the longest x2 2.78 us: rotate(): lax.ppermute(value, axis, [(i, (i + step) % size) for i in range(size)])]
  transfers between devices with their start and end apart: 10 -> 6, of which waited for: 5 -> 2; matrix products, arithmetic and copies ran while one was open for 8% -> 5% of each run, Pallas kernels for 0% -> 21%
where the time goes in v1:
time: 39.2 us; the launch traced here: 38.8 us
  Pallas kernels  19.5 us (50%)
  starting transfers between devices  10.9 us (28%)
  local copies, waits for them, and re-layouts  5.48 us (14%)
  waiting for transfers between devices  2.79 us (7%)
    pallas_call x1, Pallas kernels, local_of(): pl.pallas_call(functools.partial(local_kernel, widths, kinds), out_shape=...  10.1 us
    pallas_call x1, Pallas kernels, count_entries(): pl.pallas_call(functools.partial(count_kernel, widths, kinds, columns), o...  7.86 us
    ppermute x4, starting transfers between devices, partner(): lax.ppermute(value, axis, [(i, i ^ 1 << apart) for i in range(lax.axis_si...  6.29 us
    ppermute x2, starting transfers between devices, rotate(): lax.ppermute(value, axis, [(i, (i + step) % size) for i in range(size)])  4.62 us
    unnamed x16, local copies, waits for them, and re-layouts  3.88 us
    ppermute x2, waiting for transfers between devices, rotate(): lax.ppermute(value, axis, [(i, (i + step) % size) for i in range(size)])  2.78 us
    pallas_call x2, Pallas kernels, evaluate(): pl.pallas_call(kernel, out_shape=jax.ShapeDtypeStruct((slots, columns), j...  1.5 us
    dynamic_slice x1, local copies, waits for them, and re-layouts, share(): lax.dynamic_slice_in_dim(fine_parts[0], fine_at, fine_size, 0)  0.88 us
  transfers between devices with their start and end apart: 6, of which 2 were waited for; matrix products, arithmetic and copies ran while one was open for 5% of the time, Pallas kernels for 21%

profile of v1, /device:TPU:0, one launch (start us, length us, event | category | flops | bytes accessed | tf_op | source)
XLA Modules:
  0.0 38.8 jit_solution(4497545351719867054)
XLA Ops:
  0.0 0.7 %dynamic-slice_bitcast_fusion.3 = (bf16[32,128]{1,0:T(8,128)(2,1)S(1)}, bf16[32,128]{1,0:T(8,128)(2,1)S(1)}) fusion(bf16[1,64,128]{2,1,0:T(8,128)(2,1)} %param.12, s32[]{:T(128)S(6)} %select_n.35, s32[]{:T(128)S(6)} %select_n.40), kind=kLoop, calls=%fused_computation.5 | loop fusion | bytes 32776 | tf_op jit(solution)/shard_map/dynamic_slice | solution.py:275
  0.7 0.9 %dynamic-slice_bitcast_fusion.1 = (bf16[256,128]{1,0:T(8,128)(2,1)S(1)}, bf16[256,128]{1,0:T(8,128)(2,1)S(1)}) fusion(bf16[1,512,128]{2,1,0:T(8,128)(2,1)} %param.11, s32[]{:T(128)S(6)} %select_n.33, s32[]{:T(128)S(6)} %select_n.38), kind=kLoop, calls=%fused_computation.3 | loop fusion | bytes 262152 | tf_op jit(solution)/shard_map/dynamic_slice | solution.py:274
  1.6 3.1 %collective-permute-start = (bf16[288,128]{1,0:T(8,128)(2,1)S(1)}, bf16[288,128]{1,0:T(8,128)(2,1)S(1)}, u32[]{:S(2)}, u32[]{:S(2)}) collective-permute-start(bf16[288,128]{1,0:T(8,128)(2,1)S(1)} %pad_maximum_fusion), channel_id=1, source_target_pairs={{0,1},{1,0},{2,3},{3,2},{4,5},{5,4},{6,7},{7,6},{8,9},{9,8},{10,11... | collective-permute-start | bytes 221192 | tf_op jit(solution)/shard_map/ppermute | solution.py:23
  4.7 0.9 %copy.12.ps_ref = s32[189,64]{1,0:T(8,128)S(1)} copy(s32[189,64]{0,1:T(8,128)} %param.16) | data formatting | bytes 96768 | tf_op args[5]
  5.6 0.9 %copy.13.po_ref = s32[189,64]{1,0:T(8,128)S(1)} copy(s32[189,64]{0,1:T(8,128)} %param.17) | data formatting | bytes 96768 | tf_op args[6]
  6.5 0.5 %collective-permute-done = bf16[288,128]{1,0:T(8,128)(2,1)S(1)} collective-permute-done((bf16[288,128]{1,0:T(8,128)(2,1)S(1)}, bf16[288,128]{1,0:T(8,128)(2,1)S(1)}, u32[]{:S(2)}, u32[]{:S(2)}) %collective-permute-start) | collective-permute-done | bytes 73760 | tf_op jit(solution)/shard_map/ppermute | solution.py:23
  7.0 0.1 collective-permute-start.1
  7.1 2.1 %collective-permute-start.2 = (bf16[288,128]{1,0:T(8,128)(2,1)S(1)}, bf16[288,128]{1,0:T(8,128)(2,1)S(1)}, u32[]{:S(2)}, u32[]{:S(2)}) collective-permute-start(bf16[288,128]{1,0:T(8,128)(2,1)S(1)} %add_convert_fusion.refs_0_), channel_id=1, source_target_pairs={{0,4},{2,6},{4,0},{6,2},{8,12},{10,14},{12,8},{14,10},{16,20},{18,... | collective-permute-start | bytes 221192 | tf_op jit(solution)/shard_map/ppermute | solution.py:27
  9.2 1.6 %collective-permute-start.3 = (bf16[288,128]{1,0:T(8,128)(2,1)S(1)}, bf16[288,128]{1,0:T(8,128)(2,1)S(1)}, u32[]{:S(2)}, u32[]{:S(2)}) collective-permute-start(bf16[288,128]{1,0:T(8,128)(2,1)S(1)} %add_convert_fusion.refs_0_), channel_id=1, source_target_pairs={{0,8},{2,10},{4,12},{6,14},{8,0},{10,2},{12,4},{14,6},{16,24},{18,... | collective-permute-start | bytes 221192 | tf_op jit(solution)/shard_map/ppermute | solution.py:27
  10.7 2.6 %collective-permute-start.4 = (bf16[288,128]{1,0:T(8,128)(2,1)S(1)}, bf16[288,128]{1,0:T(8,128)(2,1)S(1)}, u32[]{:S(2)}, u32[]{:S(2)}) collective-permute-start(bf16[288,128]{1,0:T(8,128)(2,1)S(1)} %add_convert_fusion.refs_0_), channel_id=1, source_target_pairs={{0,16},{2,18},{4,20},{6,22},{8,24},{10,26},{12,28},{14,30},{16,0},... | collective-permute-start | bytes 221192 | tf_op jit(solution)/shard_map/ppermute | solution.py:27
  13.3 0.0 copy-start.3
  13.3 1.0 %copy-done.3 = s32[189,512]{1,0:T(8,128)S(1)} copy-done((s32[189,512]{1,0:T(8,128)S(1)}, s32[189,512]{1,0:T(8,128)}, u32[]{:S(2)}) %copy-start.3) | copy-done | bytes 387096
  14.3 0.0 copy-start.4
  14.3 1.0 %copy-done.4 = s32[189,512]{1,0:T(8,128)S(1)} copy-done((s32[189,512]{1,0:T(8,128)S(1)}, s32[189,512]{1,0:T(8,128)}, u32[]{:S(2)}) %copy-start.4) | copy-done | bytes 387096
  15.3 0.0 copy-start.2
  15.3 0.0 copy-start.5
  15.3 0.0 copy-start.6
  15.3 7.9 %counts.1.count_ref = bf16[18432,160]{1,0:T(8,128)(2,1)S(1)} custom-call(s32[1]{0:T(128)} %bitcast.member_ref, s32[189,512]{1,0:T(8,128)S(1)} %copy-done.3, s32[189,512]{1,0:T(8,128)S(1)} %copy-done.4, s32[189,64]{1,0:T(8,128)S(1)} %copy.12.ps_ref, s32[189,64]{1,0:T(8,128)S(1)} %copy.13.po_ref), custom_call_target="tpu_custom_call" | custom-call | flops 6039797760 | bytes 5898240 | tf_op jit(solution)/shard_map/counts/pallas_call | solution.py:88
  23.2 0.0 collective-permute-done.1.refs_1_
  23.2 0.0 collective-permute-done.2.refs_2_
  23.2 0.0 collective-permute-done.3.refs_3_
  23.2 0.0 collective-permute-done.4.refs_4_
  23.2 0.0 copy-done.2
  23.3 0.0 copy-done.5
  23.3 0.0 copy-done.6
  23.3 0.0 copy-start
  23.3 0.0 copy-start.1
  23.3 10.1 %far.1.local_ref = bf16[256,128]{1,0:T(8,128)(2,1)S(1)} custom-call(s32[1]{0:T(128)} %bitcast.member_ref, bf16[18432,160]{1,0:T(8,128)(2,1)S(1)} %counts.1.count_ref, bf16[288,128]{1,0:T(8,128)(2,1)S(1)} %add_convert_fusion.refs_0_, bf16[288,128]{1,0:T(8,128)(2,1)S(1)} %collective-permute-done.1.refs_1_, ...), custom_call_target="tpu_custom_call" | custom-call | flops 4831838208 | bytes 9437184 | tf_op jit(solution)/shard_map/far/pallas_call | solution.py:171
  33.4 1.6 %collective-permute-start.5 = (bf16[256,128]{1,0:T(8,128)(2,1)S(1)}, bf16[256,128]{1,0:T(8,128)(2,1)S(1)}, u32[]{:S(2)}, u32[]{:S(2)}) collective-permute-start(bf16[256,128]{1,0:T(8,128)(2,1)S(1)} %far.1.local_ref), channel_id=1, source_target_pairs={{0,1},{1,0},{2,3},{3,2},{4,5},{5,4},{6,7},{7,6},{8,9},{9,8},{10,11... | collective-permute-start | bytes 196616 | tf_op jit(solution)/shard_map/ppermute | solution.py:23
  35.0 0.0 copy-done
  35.0 0.0 copy-done.1
  35.0 0.4 %slots.2.own_ref = f32[16,256]{1,0:T(8,128)S(1)} custom-call(s32[1]{0:T(128)} %bitcast.member_ref, bf16[256,128]{1,0:T(8,128)(2,1)S(1)} %far.1.local_ref, bf16[512,16,128]{2,1,0:T(8,128)(2,1)S(1)} %copy-done, s32[1,512]{1,0:T(1,128)S(1)} %copy-done.1), custom_call_target="tpu_custom_call" | custom-call | flops 268435456 | bytes 1048576 | tf_op jit(solution)/shard_map/slots/pallas_call | solution.py:233
  35.4 2.3 %collective-permute-done.5.local_ref = bf16[256,128]{1,0:T(8,128)(2,1)S(1)} collective-permute-done((bf16[256,128]{1,0:T(8,128)(2,1)S(1)}, bf16[256,128]{1,0:T(8,128)(2,1)S(1)}, u32[]{:S(2)}, u32[]{:S(2)}) %collective-permute-start.5) | collective-permute-done | bytes 65568 | tf_op jit(solution)/shard_map/ppermute | solution.py:23
  37.7 1.1 %slots.3 = f32[16,512]{1,0:T(8,128)} custom-call(s32[1]{0:T(128)} %bitcast.member_ref, bf16[256,128]{1,0:T(8,128)(2,1)S(1)} %collective-permute-done.5.local_ref, bf16[512,16,128]{2,1,0:T(8,128)(2,1)S(1)} %copy-done, s32[1,512]{1,0:T(1,128)S(1)} %copy-done.1, f32[16,256]{1,0:T(8,128)S(1)} %slots.2.own_ref), custom_call_target="tpu_custom_call" | custom-call | flops 268435456 | bytes 1048576 | tf_op jit(solution)/shard_map/slots/pallas_call | solution.py:233
  (2 shorter events, 0.0 us)
Async XLA Ops:
  1.6 5.4 %collective-permute-start = (bf16[288,128]{1,0:T(8,128)(2,1)S(1)}, bf16[288,128]{1,0:T(8,128)(2,1)S(1)}, u32[]{:S(2)}, u32[]{:S(2)}) collective-permute-start(bf16[288,128]{1,0:T(8,128)(2,1)S(1)} %pad_maximum_fusion), channel_id=1, source_target_pairs={{0,1},{1,0},{2,3},{3,2},{4,5},{5,4},{6,7},{7,6},{8,9},{9,8},{10,11... | collective-permute-start | bytes 221192 | tf_op jit(solution)/shard_map/ppermute | solution.py:23
  7.0 16.2 %collective-permute-start.1 = (bf16[288,128]{1,0:T(8,128)(2,1)S(1)}, bf16[288,128]{1,0:T(8,128)(2,1)S(1)}, u32[]{:S(2)}, u32[]{:S(2)}) collective-permute-start(bf16[288,128]{1,0:T(8,128)(2,1)S(1)} %add_convert_fusion.refs_0_), channel_id=1, source_target_pairs={{0,2},{2,0},{4,6},{6,4},{8,10},{10,8},{12,14},{14,12},{16,18},{18,... | collective-permute-start | bytes 221192 | tf_op jit(solution)/shard_map/ppermute | solution.py:27
  7.1 16.1 %collective-permute-start.2 = (bf16[288,128]{1,0:T(8,128)(2,1)S(1)}, bf16[288,128]{1,0:T(8,128)(2,1)S(1)}, u32[]{:S(2)}, u32[]{:S(2)}) collective-permute-start(bf16[288,128]{1,0:T(8,128)(2,1)S(1)} %add_convert_fusion.refs_0_), channel_id=1, source_target_pairs={{0,4},{2,6},{4,0},{6,2},{8,12},{10,14},{12,8},{14,10},{16,20},{18,... | collective-permute-start | bytes 221192 | tf_op jit(solution)/shard_map/ppermute | solution.py:27
  9.2 14.1 %collective-permute-start.3 = (bf16[288,128]{1,0:T(8,128)(2,1)S(1)}, bf16[288,128]{1,0:T(8,128)(2,1)S(1)}, u32[]{:S(2)}, u32[]{:S(2)}) collective-permute-start(bf16[288,128]{1,0:T(8,128)(2,1)S(1)} %add_convert_fusion.refs_0_), channel_id=1, source_target_pairs={{0,8},{2,10},{4,12},{6,14},{8,0},{10,2},{12,4},{14,6},{16,24},{18,... | collective-permute-start | bytes 221192 | tf_op jit(solution)/shard_map/ppermute | solution.py:27
  10.7 12.5 %collective-permute-start.4 = (bf16[288,128]{1,0:T(8,128)(2,1)S(1)}, bf16[288,128]{1,0:T(8,128)(2,1)S(1)}, u32[]{:S(2)}, u32[]{:S(2)}) collective-permute-start(bf16[288,128]{1,0:T(8,128)(2,1)S(1)} %add_convert_fusion.refs_0_), channel_id=1, source_target_pairs={{0,16},{2,18},{4,20},{6,22},{8,24},{10,26},{12,28},{14,30},{16,0},... | collective-permute-start | bytes 221192 | tf_op jit(solution)/shard_map/ppermute | solution.py:27
  13.3 1.0 %copy-start.3 = (s32[189,512]{1,0:T(8,128)S(1)}, s32[189,512]{1,0:T(8,128)}, u32[]{:S(2)}) copy-start(s32[189,512]{1,0:T(8,128)} %fs_ref.1) | copy-start | bytes 1161220
  14.3 1.0 %copy-start.4 = (s32[189,512]{1,0:T(8,128)S(1)}, s32[189,512]{1,0:T(8,128)}, u32[]{:S(2)}) copy-start(s32[189,512]{1,0:T(8,128)} %fo_ref.1) | copy-start | bytes 1161220
  15.3 7.9 %copy-start.2 = (bf16[64,128,128]{2,1,0:T(8,128)(2,1)S(1)}, bf16[64,128,128]{2,1,0:T(8,128)(2,1)}, u32[]{:S(2)}) copy-start(bf16[64,128,128]{2,1,0:T(8,128)(2,1)} %param.18) | copy-start | bytes 6291460
  15.3 7.9 %copy-start.5 = (bf16[8,128,128]{2,1,0:T(8,128)(2,1)S(1)}, bf16[8,128,128]{2,1,0:T(8,128)(2,1)}, u32[]{:S(2)}) copy-start(bf16[8,128,128]{2,1,0:T(8,128)(2,1)} %refs_7_.1) | copy-start | bytes 786436
  15.3 7.9 %copy-start.6 = (f32[64,128]{1,0:T(8,128)S(1)}, f32[64,128]{1,0:T(8,128)}, u32[]{:S(2)}) copy-start(f32[64,128]{1,0:T(8,128)} %refs_6_.1) | copy-start | bytes 98308
  23.3 11.7 %copy-start = (bf16[512,16,128]{2,1,0:T(8,128)(2,1)S(1)}, bf16[512,16,128]{2,1,0:T(8,128)(2,1)}, u32[]{:S(2)}) copy-start(bf16[512,16,128]{2,1,0:T(8,128)(2,1)} %basis_ref.3) | copy-start | bytes 6291460
  23.3 11.7 %copy-start.1 = (s32[1,512]{1,0:T(1,128)S(1)}, s32[1,512]{1,0:T(1,128)}, u32[]{:S(2)}) copy-start(s32[1,512]{1,0:T(1,128)} %counts_ref.3) | copy-start | bytes 6148
  33.4 4.3 %collective-permute-start.5 = (bf16[256,128]{1,0:T(8,128)(2,1)S(1)}, bf16[256,128]{1,0:T(8,128)(2,1)S(1)}, u32[]{:S(2)}, u32[]{:S(2)}) collective-permute-start(bf16[256,128]{1,0:T(8,128)(2,1)S(1)} %far.1.local_ref), channel_id=1, source_target_pairs={{0,1},{1,0},{2,3},{3,2},{4,5},{5,4},{6,7},{7,6},{8,9},{9,8},{10,11... | collective-permute-start | bytes 196616 | tf_op jit(solution)/shard_map/ppermute | solution.py:23

commit v2 on v1

--- a/solution.py
+++ b/solution.py
@@ -27,43 +27,84 @@
     return lax.ppermute(value, axis, [(i, i ^ 1 << apart) for i in range(lax.axis_size(axis))])
 
 
-def count_kernel(
-    widths, kinds, columns, member_ref, fs_ref, fo_ref, ps_ref, po_ref, out_ref, *scratch
-):
+def pack_kernel(widths, member_ref, fine_ref, parent_ref, *refs):
+    lists, outs, sem = refs[:4], refs[4:-1], refs[-1]
     member = member_ref[0]
+    fine, parent = widths
+    copies = []
+    for at, out in ((member, outs[0]), (1 - member, outs[1])):
+        for ref, width, row in ((fine_ref, fine, 0), (parent_ref, parent, fine)):
+            start = pl.multiple_of(at * width, WINDOW)
+            copies.append((ref.at[0, pl.ds(start, width), :], out.at[pl.ds(row, width), :]))
+    lanes = pl.ds(pl.multiple_of(member * fine, LANES), fine)
+    copies += [(ref.at[:, lanes], out) for ref, out in zip(lists[:2], outs[2:4])]
+    boxes = pl.ds(pl.multiple_of(member * parent, 8), parent)
+    copies += [(ref.at[boxes, :], out) for ref, out in zip(lists[2:], outs[4:])]
+    copies = [pltpu.make_async_copy(*pair, sem.at[i]) for i, pair in enumerate(copies)]
+    for copy in copies:
+        copy.start()
+    for copy in copies:
+        copy.wait()
+
+
+def pack(member, fine_parts, parent_parts, lists, widths):
+    in_place = pl.BlockSpec(memory_space=pltpu.HBM)
+    length = lists[0].shape[0]
+    coef = fine_parts.shape[2]
+    chunk = jax.ShapeDtypeStruct((sum(widths), coef), fine_parts.dtype)
+    mine = jax.ShapeDtypeStruct((length, widths[0]), jnp.int32)
+    parents = jax.ShapeDtypeStruct((widths[1], length), jnp.int32)
+    shapes = [chunk, chunk, mine, mine, parents, parents]
+    return pl.pallas_call(
+        functools.partial(pack_kernel, widths),
+        out_shape=shapes,
+        in_specs=[SMEM] + [in_place] * 6,
+        out_specs=[VMEM] * 6,
+        scratch_shapes=[pltpu.SemaphoreType.DMA((8,))],
+        compiler_params=pltpu.CompilerParams(vmem_limit_bytes=4 << 20),
+        name="pack",
+    )(
+        member,
+        *(
+            pltpu.with_memory_space_constraint(each, pltpu.HBM)
+            for each in (fine_parts, parent_parts, *lists)
+        ),
+    )
+
+
+def count_kernel(levels, kinds, columns, *refs):
+    lists, out_ref, scratch = refs[: 2 * len(levels)], refs[-1 - 2 * len(levels)], refs[-2 * len(levels) :]
     depth = scratch[0].shape[1]
-    half = jnp.bfloat16
-    rows_iota = lax.broadcasted_iota(jnp.int32, (16, depth), 0).astype(half)
-    one = jnp.ones((), half)
-    zero = jnp.zeros((), half)
+    half, quarter = jnp.bfloat16, jnp.float8_e4m3fn
+    rows_iota = lax.broadcasted_iota(jnp.int32, (32, depth), 0).astype(half)
+    one = jnp.ones((), quarter)
+    zero = jnp.zeros((), quarter)
 
     def hot(row_ref, row, size):
-        values = jnp.broadcast_to(row_ref[pl.ds(row, 1), :], (16, depth)).astype(half)
-        pieces = [jnp.where(values == rows_iota + 16 * k, one, zero) for k in range(size // 16)]
-        return jnp.concatenate(pieces, 0).astype(jnp.float8_e4m3fn)
+        values = jnp.broadcast_to(row_ref[pl.ds(row, 1), :], (32, depth)).astype(half)
+        pieces = [jnp.where(values == rows_iota + 32 * k, one, zero) for k in range(size // 32)]
+        return jnp.concatenate(pieces, 0)
 
     done = 0
-    for (source_ref, kind_ref), (source_rows, kind_rows), width in zip(
-        ((fs_ref, fo_ref), (ps_ref, po_ref)), (scratch[:2], scratch[2:]), widths
-    ):
-        length, total = source_ref.shape
-        whole = length // 8 * 8
-        span = width if width % LANES == 0 else total
-        offset = 0 if span == width else member * width
-        for ref, rows in ((source_ref, source_rows), (kind_ref, kind_rows)):
-            if span == total:
-                body, tail = ref[:whole, :], ref[whole:, :]
-            else:
-                lanes = pl.ds(pl.multiple_of(member * width, LANES), width)
-                body, tail = ref[:whole, lanes], ref[whole:, lanes]
+    for level, (first, width, by_box) in enumerate(levels):
+        pair = slice(2 * level, 2 * level + 2)
+        for ref, rows in zip(lists[pair], scratch[pair]):
+            if by_box:
+                rows[...] = jnp.full(rows.shape, -1, jnp.float32)
+                rows[:, : ref.shape[1]] = ref[first : first + width, :].astype(jnp.float32)
+                continue
+            length, total = ref.shape
+            whole = length // 8 * 8
+            begin = first // LANES * LANES
+            span = min(rows.shape[0], total - begin)
+            lanes = slice(begin, begin + span)
             pad = jnp.full((depth - length, span), -1, jnp.int32)
-            entries = jnp.concatenate([body, tail, pad], 0).astype(jnp.float32)
-            extra = rows.shape[0] - span
-            if extra:
-                entries = jnp.concatenate([entries, jnp.zeros((depth, extra), jnp.float32)], 1)
-            rows[...] = entries.T
-
-        def one_box(box, _, offset=offset, done=done, source_rows=source_rows, kind_rows=kind_rows):
+            entries = jnp.concatenate([ref[:whole, lanes], ref[whole:, lanes], pad], 0)
+            rows[...] = entries.astype(jnp.float32).T
+        source_rows, kind_rows = scratch[pair]
+        offset = 0 if by_box else first % LANES
+
+        def one_box(box, _):
             source_hot = hot(source_rows, box + offset, columns)
             kind_hot = hot(kind_rows, box + offset, kinds)
             counted = lax.dot_general(
@@ -73,82 +114,67 @@
             out_ref[pl.ds(start, kinds), :] = counted.astype(half)
             return 0
 
-        lax.fori_loop(0, width, one_box, 0, unroll=8)
+        lax.fori_loop(0, width, one_box, 0, unroll=min(width, 64))
         done += width
 
 
-def count_entries(member, fine_source, fine_kind, parent_source, parent_kind, widths, kinds, columns):
-    length = fine_source.shape[0]
+def count_entries(lists, length, levels, kinds, columns, after=()):
     depth = round_up(length, LANES)
-    boxes = sum(widths)
+    boxes = sum(width for _, width, _ in levels)
     scratch = []
-    for source, width in ((fine_source, widths[0]), (parent_source, widths[1])):
-        span = width if width % LANES == 0 else source.shape[1]
-        scratch += [pltpu.VMEM((round_up(span, LANES), depth), jnp.float32)] * 2
+    for first, width, by_box in levels:
+        span = width if by_box else round_up(first % LANES + width, LANES)
+        scratch += [pltpu.VMEM((span, depth), jnp.float32)] * 2
     return pl.pallas_call(
-        functools.partial(count_kernel, widths, kinds, columns),
+        functools.partial(count_kernel, levels, kinds, columns),
         out_shape=jax.ShapeDtypeStruct((boxes * kinds, columns), jnp.bfloat16),
-        in_specs=[SMEM] + [VMEM] * 4,
+        in_specs=[VMEM] * (len(lists) + len(after)),
         out_specs=VMEM,
         scratch_shapes=scratch,
-        compiler_params=pltpu.CompilerParams(vmem_limit_bytes=24 << 20),
+        compiler_params=pltpu.CompilerParams(vmem_limit_bytes=8 << 20),
         cost_estimate=pl.CostEstimate(
             flops=2 * boxes * depth * kinds * columns * 4,
             bytes_accessed=boxes * kinds * columns * 2,
             transcendentals=0,
         ),
         name="counts",
-    )(member, fine_source, fine_kind, parent_source, parent_kind)
-
-
-def local_kernel(
-    widths, kinds, member_ref, count_ref, *refs
-):
+    )(*lists, *after)
+
+
+def local_kernel(widths, firsts, kinds, member_ref, *refs):
+    counted, refs = refs[: len(firsts)], refs[len(firsts) :]
     (b0, b1, b2, b3, b4, ops_ref, coarse_ref, shift_ref, out_ref, grouped, total, moved) = refs
     blocks = (b0, b1, b2, b3, b4)
     member = member_ref[0]
     fine, parent = widths
+    boxes = fine + parent
     coef = out_ref.shape[1]
-    rows = WINDOW * kinds
-
-    def one_window(window, _):
-        start = pl.multiple_of(window * WINDOW, WINDOW)
-        nearby = jnp.concatenate([ref[pl.ds(start, WINDOW), :] for ref in blocks], 0)
-        at = pl.multiple_of(window * rows, rows)
-        grouped[pl.ds(at, rows), :] = jnp.dot(
-            count_ref[pl.ds(at, rows), :], nearby, preferred_element_type=jnp.float32
+    pitch = grouped.shape[0] // boxes
+
+    for start in range(0, boxes, WINDOW):
+        count = min(WINDOW, boxes - start)
+        nearby = jnp.concatenate([ref[start : start + WINDOW, :] for ref in blocks], 0)
+        which = max(i for i in range(len(firsts)) if firsts[i] <= start)
+        at = (start - firsts[which]) * kinds
+        values = jnp.dot(
+            counted[which][at : at + count * kinds, :], nearby, preferred_element_type=jnp.float32
         )
-        return 0
-
-    lax.fori_loop(0, fine // WINDOW, one_window, 0)
-    spread = max(parent, WINDOW)
-    for piece in range(spread // WINDOW):
-        start = fine + piece * WINDOW
-        nearby = jnp.concatenate([ref[start : start + WINDOW, :] for ref in blocks], 0)
-        count = min(parent, WINDOW) * kinds
-        at = (fine + piece * WINDOW) * kinds
-        grouped[at : at + count, :] = jnp.dot(
-            count_ref[at : at + count, :], nearby, preferred_element_type=jnp.float32
-        )
-
-    boxes = fine + parent
+        for box in range(count):
+            row = (start + box) * pitch
+            grouped[row : row + kinds, :] = values[box * kinds : (box + 1) * kinds]
+
     step = 8
-    total[...] = jnp.zeros_like(total)
-
-    def some_kinds(at, _):
+    for at in range(0, kinds, step):
         picked = [
-            grouped[pl.ds(at * step + k, boxes, stride=kinds), :].astype(jnp.bfloat16)
+            grouped[pl.ds(at + k, boxes, stride=pitch), :].astype(jnp.bfloat16)
             for k in range(step)
         ]
-        start = pl.multiple_of(at * step * coef, step * coef)
-        total[...] += jnp.dot(
+        term = jnp.dot(
             jnp.concatenate(picked, 1),
-            ops_ref[pl.ds(start, step * coef), :],
+            ops_ref[at * coef : (at + step) * coef, :],
             preferred_element_type=jnp.float32,
         )
-        return 0
-
-    lax.fori_loop(0, kinds // step, some_kinds, 0)
+        total[...] = term + total[...] if at else term
     begin = member * parent
     if parent % 8 == 0:
         begin = pl.multiple_of(begin, 8)
@@ -164,28 +190,28 @@
     out_ref[...] = jnp.where(keep, whole, 0.0).astype(jnp.bfloat16)
 
 
-def local_of(member, counted, blocks, flat_ops, coarse, child_shift, widths, kinds):
+def local_of(member, counted, firsts, blocks, flat_ops, coarse, child_shift, widths, kinds):
     fine, parent = widths
     coef = flat_ops.shape[1]
     boxes = fine + parent
     return pl.pallas_call(
-        functools.partial(local_kernel, widths, kinds),
+        functools.partial(local_kernel, widths, firsts, kinds),
         out_shape=jax.ShapeDtypeStruct((fine, coef), jnp.bfloat16),
-        in_specs=[SMEM] + [VMEM] * 9,
+        in_specs=[SMEM] + [VMEM] * (8 + len(counted)),
         out_specs=VMEM,
         scratch_shapes=[
-            pltpu.VMEM((boxes * kinds, coef), jnp.float32),
+            pltpu.VMEM((boxes * (kinds + 4), coef), jnp.float32),
             pltpu.VMEM((boxes, coef), jnp.float32),
             pltpu.VMEM((fine, coef), jnp.float32),
         ],
-        compiler_params=pltpu.CompilerParams(vmem_limit_bytes=32 << 20),
+        compiler_params=pltpu.CompilerParams(vmem_limit_bytes=24 << 20),
         cost_estimate=pl.CostEstimate(
             flops=8 * boxes * kinds * coef * 256,
             bytes_accessed=boxes * kinds * coef * 4,
             transcendentals=0,
         ),
         name="far",
-    )(member, counted, *blocks, flat_ops, coarse, child_shift)
+    )(member, *counted, *blocks, flat_ops, coarse, child_shift)
 
 
 def slots_of(basis_ref, counts_ref, box, local):
@@ -265,6 +291,9 @@
     widths = (fine_total // group, parent_total // group)
     index = member.astype(jnp.int32).reshape(1)
 
+    lists = (fine_source, fine_operator, parent_source.T, parent_operator.T)
+    special = group == 2 and widths[0] % (2 * LANES) == 0 and widths[1] % WINDOW == 0
+
     def share(whose):
         fine_size, parent_size = max(widths[0], WINDOW), max(widths[1], WINDOW)
         fine_at = whose * widths[0] // WINDOW * WINDOW
@@ -277,24 +306,39 @@
             0,
         )
 
-    summed = share(member).astype(jnp.float32)
-    for step in range(1, group):
-        summed += rotate(share((member + step) % group), "batch", step).astype(jnp.float32)
-    own = summed.astype(jnp.bfloat16)
+    columns = 5 * WINDOW
+    length = fine_source.shape[0]
+    if special:
+        mine, theirs, *lists = pack(index, fine_parts, parent_parts, lists, widths)
+        early = widths[0] // 2
+        late = widths[0] - early
+        counted_late = ((early, late, False), (0, widths[1], True))
+        summed = mine.astype(jnp.float32) + rotate(theirs, "batch", 1).astype(jnp.float32)
+        own = summed.astype(jnp.bfloat16)
+        counted = [
+            count_entries(lists[:2], length, ((0, early, False),), kinds, columns),
+            count_entries(lists, length, counted_late, kinds, columns, (own,)),
+        ]
+        firsts = (0, early)
+    else:
+        summed = share(member).astype(jnp.float32)
+        for step in range(1, group):
+            summed += rotate(share((member + step) % group), "batch", step).astype(jnp.float32)
+        own = summed.astype(jnp.bfloat16)
+        levels = ((0, widths[0], True), (0, widths[1], True))
+        lists = [
+            lax.dynamic_slice_in_dim(each, member * width, width, 0)
+            for each, width in zip(
+                (fine_source.T, fine_operator.T, *lists[2:]), (*widths[:1] * 2, *widths[1:] * 2)
+            )
+        ]
+        counted = [count_entries(lists, length, levels, kinds, columns)]
+        firsts = (0,)
     blocks = [own] + [partner(own, "space", bit) for bit in range(4)]
-    counted = count_entries(
-        index,
-        fine_source,
-        fine_operator,
-        parent_source,
-        parent_operator,
-        widths,
-        kinds,
-        5 * WINDOW,
-    )
     local = local_of(
         index,
         counted,
+        firsts,
         blocks,
         operators.reshape(kinds * coef, coef),
         coarse_local,
@@ -302,7 +346,7 @@
         widths,
         kinds,
     )
-    if group == 2 and widths[0] % LANES == 0:
+    if special:
         other = rotate(local, "batch", 1)
         mine = evaluate(own_kernel, widths[0], index, local, basis, counts)
         return evaluate(other_kernel, fine_total, index, other, basis, counts, mine)

time: 39.2 us -> 27.2 us (0.69)
  Pallas kernels: 19.5 us -> 11.3 us
  local copies, waits for them, and re-layouts: 5.48 us -> 0.02 us
  waiting for transfers between devices: 2.79 us -> 4.66 us
    pallas_call x2 -> x4, Pallas kernels: 18 us -> 9.81 us  [the longest x1 4.7 us: local_of(): pl.pallas_call(functools.partial(local_kernel, widths, firsts, kinds), ou...]
    unnamed x16 -> x10, local copies, waits for them, and re-layouts: 3.88 us -> 0.02 us
    ppermute x4, waiting for transfers between devices: 0.01 us -> 1.77 us  [partner(): lax.ppermute(value, axis, [(i, i ^ 1 << apart) for i in range(lax.axis_si...]
    dynamic_slice x2 -> x0, local copies, waits for them, and re-layouts: 1.6 us -> none  [the longest x1 0.88 us: share(): lax.dynamic_slice_in_dim(fine_parts[0], fine_at, fine_size, 0)]
  transfers between devices with their start and end apart: 6 -> 6, of which waited for: 2 -> 3; matrix products, arithmetic and copies ran while one was open for 5% -> 0% of each run, Pallas kernels for 21% -> 16%
where the time goes in v2:
time: 27.2 us; the launch traced here: 27 us
  Pallas kernels  11.3 us (42%)
  starting transfers between devices  10.9 us (40%)
  waiting for transfers between devices  4.66 us (17%)
    ppermute x4, starting transfers between devices, partner(): lax.ppermute(value, axis, [(i, i ^ 1 << apart) for i in range(lax.axis_si...  6.29 us
    pallas_call x1, Pallas kernels, local_of(): pl.pallas_call(functools.partial(local_kernel, widths, firsts, kinds), ou...  4.7 us
    ppermute x2, starting transfers between devices, rotate(): lax.ppermute(value, axis, [(i, (i + step) % size) for i in range(size)])  4.64 us
    pallas_call x2, Pallas kernels, count_entries(): pl.pallas_call(functools.partial(count_kernel, levels, kinds, columns), o...  3.91 us
    ppermute x2, waiting for transfers between devices, rotate(): lax.ppermute(value, axis, [(i, (i + step) % size) for i in range(size)])  2.9 us
    ppermute x4, waiting for transfers between devices, partner(): lax.ppermute(value, axis, [(i, i ^ 1 << apart) for i in range(lax.axis_si...  1.77 us
    pallas_call x2, Pallas kernels, evaluate(): pl.pallas_call(kernel, out_shape=jax.ShapeDtypeStruct((slots, columns), j...  1.49 us
    pallas_call x1, Pallas kernels, pack(): pl.pallas_call(functools.partial(pack_kernel, widths), out_shape=shapes,...  1.2 us
  transfers between devices with their start and end apart: 6, of which 3 were waited for; matrix products, arithmetic and copies ran while one was open for 0% of the time, Pallas kernels for 16%

profile of v2, /device:TPU:0, one launch (start us, length us, event | category | flops | bytes accessed | tf_op | source)
XLA Modules:
  0.0 27.0 jit_solution(14791022137103430309)
XLA Ops:
  0.0 1.2 %pack.1 = (bf16[288,128]{1,0:T(8,128)(2,1)S(1)}, bf16[288,128]{1,0:T(8,128)(2,1)S(1)}, s32[189,256]{1,0:T(8,128)S(1)}, s32[189,256]{1,0:T(8,128)S(1)}, s32[32,189]{1,0:T(8,128)S(1)}, /*index=5*/s32[32,189]{1,0:T(8,128)S(1)}) custom-call(s32[1]{0:T(128)} %bitcast.member_ref, bf16[1,512,128]{2,1,0:T(8,128)(2,1)} %fine_ref.1, bf16[1,64,128]{2,1,0:T(8,128)(2,1)} %parent_ref.1, ...), custom_call_target="tpu_custom_call" | custom-call | tf_op jit(solution)/shard_map/pack/pallas_call | solution.py:58
  1.2 3.1 %collective-permute-start = (bf16[288,128]{1,0:T(8,128)(2,1)S(1)}, bf16[288,128]{1,0:T(8,128)(2,1)S(1)}, u32[]{:S(2)}, u32[]{:S(2)}) collective-permute-start(bf16[288,128]{1,0:T(8,128)(2,1)S(1)} %get-tuple-element.16), channel_id=1, source_target_pairs={{0,1},{1,0},{2,3},{3,2},{4,5},{5,4},{6,7},{7,6},{8,9},{9,8},{10,11... | collective-permute-start | bytes 221192 | tf_op jit(solution)/shard_map/ppermute | solution.py:23
  4.3 1.7 %counts.2.refs_0_ = bf16[8192,160]{1,0:T(8,128)(2,1)S(1)} custom-call(s32[189,256]{1,0:T(8,128)S(1)} %get-tuple-element.11.refs_0_, s32[189,256]{1,0:T(8,128)S(1)} %get-tuple-element.12.refs_1_), custom_call_target="tpu_custom_call" | custom-call | flops 2684354560 | bytes 2621440 | tf_op jit(solution)/shard_map/counts/pallas_call | solution.py:128
  6.0 0.6 %collective-permute-done = bf16[288,128]{1,0:T(8,128)(2,1)S(1)} collective-permute-done((bf16[288,128]{1,0:T(8,128)(2,1)S(1)}, bf16[288,128]{1,0:T(8,128)(2,1)S(1)}, u32[]{:S(2)}, u32[]{:S(2)}) %collective-permute-start) | collective-permute-done | bytes 73760 | tf_op jit(solution)/shard_map/ppermute | solution.py:23
  6.6 0.1 collective-permute-start.1
  6.7 2.1 %collective-permute-start.2 = (bf16[288,128]{1,0:T(8,128)(2,1)S(1)}, bf16[288,128]{1,0:T(8,128)(2,1)S(1)}, u32[]{:S(2)}, u32[]{:S(2)}) collective-permute-start(bf16[288,128]{1,0:T(8,128)(2,1)S(1)} %add_convert_fusion.refs_4_.refs_2_), channel_id=1, source_target_pairs={{0,4},{2,6},{4,0},{6,2},{8,12},{10,14},{12,8},{14,10},{16,20},{18,... | collective-permute-start | bytes 221192 | tf_op jit(solution)/shard_map/ppermute | solution.py:27
  8.8 1.6 %collective-permute-start.3 = (bf16[288,128]{1,0:T(8,128)(2,1)S(1)}, bf16[288,128]{1,0:T(8,128)(2,1)S(1)}, u32[]{:S(2)}, u32[]{:S(2)}) collective-permute-start(bf16[288,128]{1,0:T(8,128)(2,1)S(1)} %add_convert_fusion.refs_4_.refs_2_), channel_id=1, source_target_pairs={{0,8},{2,10},{4,12},{6,14},{8,0},{10,2},{12,4},{14,6},{16,24},{18,... | collective-permute-start | bytes 221192 | tf_op jit(solution)/shard_map/ppermute | solution.py:27
  10.3 2.6 %collective-permute-start.4 = (bf16[288,128]{1,0:T(8,128)(2,1)S(1)}, bf16[288,128]{1,0:T(8,128)(2,1)S(1)}, u32[]{:S(2)}, u32[]{:S(2)}) collective-permute-start(bf16[288,128]{1,0:T(8,128)(2,1)S(1)} %add_convert_fusion.refs_4_.refs_2_), channel_id=1, source_target_pairs={{0,16},{2,18},{4,20},{6,22},{8,24},{10,26},{12,28},{14,30},{16,0},... | collective-permute-start | bytes 221192 | tf_op jit(solution)/shard_map/ppermute | solution.py:27
  12.9 0.0 copy-start.2
  12.9 0.0 copy-start.3
  12.9 0.0 copy-start.4
  12.9 2.2 %counts.3.refs_1_ = bf16[10240,160]{1,0:T(8,128)(2,1)S(1)} custom-call(s32[189,256]{1,0:T(8,128)S(1)} %get-tuple-element.11.refs_0_, s32[189,256]{1,0:T(8,128)S(1)} %get-tuple-element.12.refs_1_, s32[32,189]{1,0:T(8,128)S(1)} %get-tuple-element.13.refs_2_, s32[32,189]{1,0:T(8,128)S(1)} %get-tuple-element.14.refs_3_, ...), custom_call_target="tpu_custom_call" | custom-call | flops 3355443200 | bytes 3276800 | tf_op jit(solution)/shard_map/counts/pallas_call | solution.py:128
  15.1 0.0 collective-permute-done.1.refs_3_
  15.1 0.0 collective-permute-done.2.refs_4_
  15.1 0.0 collective-permute-done.3.refs_5_
  15.2 1.8 %collective-permute-done.4.refs_6_ = bf16[288,128]{1,0:T(8,128)(2,1)S(1)} collective-permute-done((bf16[288,128]{1,0:T(8,128)(2,1)S(1)}, bf16[288,128]{1,0:T(8,128)(2,1)S(1)}, u32[]{:S(2)}, u32[]{:S(2)}) %collective-permute-start.4) | collective-permute-done | bytes 73760 | tf_op jit(solution)/shard_map/ppermute | solution.py:27
  16.9 0.0 copy-done.2
  16.9 0.0 copy-done.3
  16.9 0.0 copy-done.4
  16.9 0.0 copy-start
  16.9 0.0 copy-start.1
  17.0 4.7 %far.1.local_ref = bf16[256,128]{1,0:T(8,128)(2,1)S(1)} custom-call(s32[1]{0:T(128)} %bitcast.member_ref, bf16[8192,160]{1,0:T(8,128)(2,1)S(1)} %counts.2.refs_0_, bf16[10240,160]{1,0:T(8,128)(2,1)S(1)} %counts.3.refs_1_, bf16[288,128]{1,0:T(8,128)(2,1)S(1)} %add_convert_fusion.refs_4_.refs_2_, bf16[288,128]{1,0:T(8,128)(2,1)S(1)} %collective-permute-done.1.refs_3_, ...), custom_call_target="tpu_custom_call" | custom-call | flops 4831838208 | bytes 9437184 | tf_op jit(solution)/shard_map/far/pallas_call | solution.py:197
  21.7 1.6 %collective-permute-start.5 = (bf16[256,128]{1,0:T(8,128)(2,1)S(1)}, bf16[256,128]{1,0:T(8,128)(2,1)S(1)}, u32[]{:S(2)}, u32[]{:S(2)}) collective-permute-start(bf16[256,128]{1,0:T(8,128)(2,1)S(1)} %far.1.local_ref), channel_id=1, source_target_pairs={{0,1},{1,0},{2,3},{3,2},{4,5},{5,4},{6,7},{7,6},{8,9},{9,8},{10,11... | collective-permute-start | bytes 196616 | tf_op jit(solution)/shard_map/ppermute | solution.py:23
  23.2 0.0 copy-done
  23.2 0.0 copy-done.1
  23.3 0.4 %slots.2.own_ref = f32[16,256]{1,0:T(8,128)S(1)} custom-call(s32[1]{0:T(128)} %bitcast.member_ref, bf16[256,128]{1,0:T(8,128)(2,1)S(1)} %far.1.local_ref, bf16[512,16,128]{2,1,0:T(8,128)(2,1)S(1)} %copy-done, s32[1,512]{1,0:T(1,128)S(1)} %copy-done.1), custom_call_target="tpu_custom_call" | custom-call | flops 268435456 | bytes 1048576 | tf_op jit(solution)/shard_map/slots/pallas_call | solution.py:259
  23.7 2.3 %collective-permute-done.5.local_ref = bf16[256,128]{1,0:T(8,128)(2,1)S(1)} collective-permute-done((bf16[256,128]{1,0:T(8,128)(2,1)S(1)}, bf16[256,128]{1,0:T(8,128)(2,1)S(1)}, u32[]{:S(2)}, u32[]{:S(2)}) %collective-permute-start.5) | collective-permute-done | bytes 65568 | tf_op jit(solution)/shard_map/ppermute | solution.py:23
  26.0 1.1 %slots.3 = f32[16,512]{1,0:T(8,128)} custom-call(s32[1]{0:T(128)} %bitcast.member_ref, bf16[256,128]{1,0:T(8,128)(2,1)S(1)} %collective-permute-done.5.local_ref, bf16[512,16,128]{2,1,0:T(8,128)(2,1)S(1)} %copy-done, s32[1,512]{1,0:T(1,128)S(1)} %copy-done.1, f32[16,256]{1,0:T(8,128)S(1)} %slots.2.own_ref), custom_call_target="tpu_custom_call" | custom-call | flops 268435456 | bytes 1048576 | tf_op jit(solution)/shard_map/slots/pallas_call | solution.py:259
  (1 shorter events, 0.0 us)
Async XLA Ops:
  1.2 5.4 %collective-permute-start = (bf16[288,128]{1,0:T(8,128)(2,1)S(1)}, bf16[288,128]{1,0:T(8,128)(2,1)S(1)}, u32[]{:S(2)}, u32[]{:S(2)}) collective-permute-start(bf16[288,128]{1,0:T(8,128)(2,1)S(1)} %get-tuple-element.16), channel_id=1, source_target_pairs={{0,1},{1,0},{2,3},{3,2},{4,5},{5,4},{6,7},{7,6},{8,9},{9,8},{10,11... | collective-permute-start | bytes 221192 | tf_op jit(solution)/shard_map/ppermute | solution.py:23
  6.6 8.5 %collective-permute-start.1 = (bf16[288,128]{1,0:T(8,128)(2,1)S(1)}, bf16[288,128]{1,0:T(8,128)(2,1)S(1)}, u32[]{:S(2)}, u32[]{:S(2)}) collective-permute-start(bf16[288,128]{1,0:T(8,128)(2,1)S(1)} %add_convert_fusion.refs_4_.refs_2_), channel_id=1, source_target_pairs={{0,2},{2,0},{4,6},{6,4},{8,10},{10,8},{12,14},{14,12},{16,18},{18,... | collective-permute-start | bytes 221192 | tf_op jit(solution)/shard_map/ppermute | solution.py:27
  6.7 8.4 %collective-permute-start.2 = (bf16[288,128]{1,0:T(8,128)(2,1)S(1)}, bf16[288,128]{1,0:T(8,128)(2,1)S(1)}, u32[]{:S(2)}, u32[]{:S(2)}) collective-permute-start(bf16[288,128]{1,0:T(8,128)(2,1)S(1)} %add_convert_fusion.refs_4_.refs_2_), channel_id=1, source_target_pairs={{0,4},{2,6},{4,0},{6,2},{8,12},{10,14},{12,8},{14,10},{16,20},{18,... | collective-permute-start | bytes 221192 | tf_op jit(solution)/shard_map/ppermute | solution.py:27
  8.8 6.4 %collective-permute-start.3 = (bf16[288,128]{1,0:T(8,128)(2,1)S(1)}, bf16[288,128]{1,0:T(8,128)(2,1)S(1)}, u32[]{:S(2)}, u32[]{:S(2)}) collective-permute-start(bf16[288,128]{1,0:T(8,128)(2,1)S(1)} %add_convert_fusion.refs_4_.refs_2_), channel_id=1, source_target_pairs={{0,8},{2,10},{4,12},{6,14},{8,0},{10,2},{12,4},{14,6},{16,24},{18,... | collective-permute-start | bytes 221192 | tf_op jit(solution)/shard_map/ppermute | solution.py:27
  10.3 6.6 %collective-permute-start.4 = (bf16[288,128]{1,0:T(8,128)(2,1)S(1)}, bf16[288,128]{1,0:T(8,128)(2,1)S(1)}, u32[]{:S(2)}, u32[]{:S(2)}) collective-permute-start(bf16[288,128]{1,0:T(8,128)(2,1)S(1)} %add_convert_fusion.refs_4_.refs_2_), channel_id=1, source_target_pairs={{0,16},{2,18},{4,20},{6,22},{8,24},{10,26},{12,28},{14,30},{16,0},... | collective-permute-start | bytes 221192 | tf_op jit(solution)/shard_map/ppermute | solution.py:27
  12.9 4.0 %copy-start.2 = (bf16[64,128,128]{2,1,0:T(8,128)(2,1)S(1)}, bf16[64,128,128]{2,1,0:T(8,128)(2,1)}, u32[]{:S(2)}) copy-start(bf16[64,128,128]{2,1,0:T(8,128)(2,1)} %param.18) | copy-start | bytes 6291460
  12.9 4.0 %copy-start.3 = (bf16[8,128,128]{2,1,0:T(8,128)(2,1)S(1)}, bf16[8,128,128]{2,1,0:T(8,128)(2,1)}, u32[]{:S(2)}) copy-start(bf16[8,128,128]{2,1,0:T(8,128)(2,1)} %refs_9_.1) | copy-start | bytes 786436
  12.9 4.0 %copy-start.4 = (f32[64,128]{1,0:T(8,128)S(1)}, f32[64,128]{1,0:T(8,128)}, u32[]{:S(2)}) copy-start(f32[64,128]{1,0:T(8,128)} %refs_8_.1) | copy-start | bytes 98308
  16.9 6.3 %copy-start = (bf16[512,16,128]{2,1,0:T(8,128)(2,1)S(1)}, bf16[512,16,128]{2,1,0:T(8,128)(2,1)}, u32[]{:S(2)}) copy-start(bf16[512,16,128]{2,1,0:T(8,128)(2,1)} %basis_ref.3) | copy-start | bytes 6291460
  16.9 6.3 %copy-start.1 = (s32[1,512]{1,0:T(1,128)S(1)}, s32[1,512]{1,0:T(1,128)}, u32[]{:S(2)}) copy-start(s32[1,512]{1,0:T(1,128)} %counts_ref.3) | copy-start | bytes 6148
  21.7 4.3 %collective-permute-start.5 = (bf16[256,128]{1,0:T(8,128)(2,1)S(1)}, bf16[256,128]{1,0:T(8,128)(2,1)S(1)}, u32[]{:S(2)}, u32[]{:S(2)}) collective-permute-start(bf16[256,128]{1,0:T(8,128)(2,1)S(1)} %far.1.local_ref), channel_id=1, source_target_pairs={{0,1},{1,0},{2,3},{3,2},{4,5},{5,4},{6,7},{7,6},{8,9},{9,8},{10,11... | collective-permute-start | bytes 196616 | tf_op jit(solution)/shard_map/ppermute | solution.py:23

commit v3 on v2

--- a/solution.py
+++ b/solution.py
@@ -7,10 +7,12 @@
 from jax.experimental.pallas import tpu as pltpu
 from jax.sharding import PartitionSpec as P
 
+
 NTERMS = 121
 WINDOW = 32
 LANES = 128
 VMEM = pl.BlockSpec(memory_space=pltpu.VMEM)
+HBM = pl.BlockSpec(memory_space=pltpu.HBM)
 SMEM = pl.BlockSpec(memory_space=pltpu.SMEM)
 
 
@@ -27,54 +29,40 @@
     return lax.ppermute(value, axis, [(i, i ^ 1 << apart) for i in range(lax.axis_size(axis))])
 
 
-def pack_kernel(widths, member_ref, fine_ref, parent_ref, *refs):
-    lists, outs, sem = refs[:4], refs[4:-1], refs[-1]
+def pack_kernel(widths, member_ref, fine_ref, parent_ref, mine_ref, theirs_ref, sem):
     member = member_ref[0]
     fine, parent = widths
     copies = []
-    for at, out in ((member, outs[0]), (1 - member, outs[1])):
+    for at, out in ((1 - member, theirs_ref), (member, mine_ref)):
         for ref, width, row in ((fine_ref, fine, 0), (parent_ref, parent, fine)):
             start = pl.multiple_of(at * width, WINDOW)
-            copies.append((ref.at[0, pl.ds(start, width), :], out.at[pl.ds(row, width), :]))
-    lanes = pl.ds(pl.multiple_of(member * fine, LANES), fine)
-    copies += [(ref.at[:, lanes], out) for ref, out in zip(lists[:2], outs[2:4])]
-    boxes = pl.ds(pl.multiple_of(member * parent, 8), parent)
-    copies += [(ref.at[boxes, :], out) for ref, out in zip(lists[2:], outs[4:])]
-    copies = [pltpu.make_async_copy(*pair, sem.at[i]) for i, pair in enumerate(copies)]
+            pair = ref.at[0, pl.ds(start, width), :], out.at[pl.ds(row, width), :]
+            copies.append(pltpu.make_async_copy(*pair, sem.at[len(copies)]))
     for copy in copies:
         copy.start()
     for copy in copies:
         copy.wait()
 
 
-def pack(member, fine_parts, parent_parts, lists, widths):
-    in_place = pl.BlockSpec(memory_space=pltpu.HBM)
-    length = lists[0].shape[0]
-    coef = fine_parts.shape[2]
-    chunk = jax.ShapeDtypeStruct((sum(widths), coef), fine_parts.dtype)
-    mine = jax.ShapeDtypeStruct((length, widths[0]), jnp.int32)
-    parents = jax.ShapeDtypeStruct((widths[1], length), jnp.int32)
-    shapes = [chunk, chunk, mine, mine, parents, parents]
+def in_place(values):
+    return [pltpu.with_memory_space_constraint(each, pltpu.HBM) for each in values]
+
+
+def pack(member, fine_parts, parent_parts, widths):
+    chunk = jax.ShapeDtypeStruct((sum(widths), fine_parts.shape[2]), fine_parts.dtype)
     return pl.pallas_call(
         functools.partial(pack_kernel, widths),
-        out_shape=shapes,
-        in_specs=[SMEM] + [in_place] * 6,
-        out_specs=[VMEM] * 6,
-        scratch_shapes=[pltpu.SemaphoreType.DMA((8,))],
+        out_shape=[chunk, chunk],
+        in_specs=[SMEM, HBM, HBM],
+        out_specs=[VMEM, VMEM],
+        scratch_shapes=[pltpu.SemaphoreType.DMA((4,))],
         compiler_params=pltpu.CompilerParams(vmem_limit_bytes=4 << 20),
         name="pack",
-    )(
-        member,
-        *(
-            pltpu.with_memory_space_constraint(each, pltpu.HBM)
-            for each in (fine_parts, parent_parts, *lists)
-        ),
-    )
-
-
-def count_kernel(levels, kinds, columns, *refs):
-    lists, out_ref, scratch = refs[: 2 * len(levels)], refs[-1 - 2 * len(levels)], refs[-2 * len(levels) :]
-    depth = scratch[0].shape[1]
+    )(member, *in_place((fine_parts, parent_parts)))
+
+
+def count_boxes(source_rows, kind_rows, first, width, kinds, columns, out_ref, done):
+    depth = source_rows.shape[1]
     half, quarter = jnp.bfloat16, jnp.float8_e4m3fn
     rows_iota = lax.broadcasted_iota(jnp.int32, (32, depth), 0).astype(half)
     one = jnp.ones((), quarter)
@@ -85,60 +73,94 @@
         pieces = [jnp.where(values == rows_iota + 32 * k, one, zero) for k in range(size // 32)]
         return jnp.concatenate(pieces, 0)
 
+    def one_box(box, _):
+        source_hot = hot(source_rows, box + first, columns)
+        kind_hot = hot(kind_rows, box + first, kinds)
+        counted = lax.dot_general(
+            kind_hot, source_hot, (((1,), (1,)), ((), ())), preferred_element_type=jnp.float32
+        )
+        start = pl.multiple_of((box + done) * kinds, kinds)
+        out_ref[pl.ds(start, kinds), :] = counted.astype(half)
+        return 0
+
+    lax.fori_loop(0, width, one_box, 0, unroll=min(width, 64))
+
+
+def first_kernel(early, kinds, columns, member_ref, *refs):
+    lists, out_ref, rows, loaded, sem = refs[:4], refs[4], refs[5:9], refs[9:13], refs[13]
+    member = member_ref[0]
+    length, fine = loaded[0].shape
+    parent = loaded[2].shape[0]
+    lanes = pl.ds(pl.multiple_of(member * fine, LANES), fine)
+    boxes = pl.ds(pl.multiple_of(member * parent, 8), parent)
+    copies = [
+        pltpu.make_async_copy(ref.at[where], out, sem.at[i])
+        for i, (ref, where, out) in enumerate(
+            zip(lists, ((slice(None), lanes),) * 2 + ((boxes, slice(None)),) * 2, loaded)
+        )
+    ]
+    for copy in copies:
+        copy.start()
+    depth = rows[0].shape[1]
+    whole = length // 8 * 8
+    pad = jnp.full((depth - length, fine), -1, jnp.int32)
+    for copy, ref, out in zip(copies[:2], loaded[:2], rows[:2]):
+        copy.wait()
+        entries = jnp.concatenate([ref[:whole, :], ref[whole:, :], pad], 0)
+        out[...] = entries.astype(jnp.float32).T
+    for copy, ref, out in zip(copies[2:], loaded[2:], rows[2:]):
+        copy.wait()
+        out[...] = jnp.full(out.shape, -1, jnp.float32)
+        out[:, :length] = ref[...].astype(jnp.float32)
+    count_boxes(*rows[:2], 0, early, kinds, columns, out_ref, 0)
+
+
+def first_counts(member, lists, widths, early, kinds, columns):
+    length = lists[0].shape[0]
+    depth = round_up(length, LANES)
+    rows = [jax.ShapeDtypeStruct((width, depth), jnp.float32) for width in widths for _ in "ab"]
+    loaded = [pltpu.VMEM((length, widths[0]), jnp.int32)] * 2
+    loaded += [pltpu.VMEM((widths[1], length), jnp.int32)] * 2
+    return pl.pallas_call(
+        functools.partial(first_kernel, early, kinds, columns),
+        out_shape=[jax.ShapeDtypeStruct((early * kinds, columns), jnp.bfloat16)] + rows,
+        in_specs=[SMEM] + [HBM] * 4,
+        out_specs=[VMEM] * 5,
+        scratch_shapes=loaded + [pltpu.SemaphoreType.DMA((4,))],
+        compiler_params=pltpu.CompilerParams(vmem_limit_bytes=8 << 20),
+        cost_estimate=count_cost(early, depth, kinds, columns),
+        name="first_counts",
+    )(member, *in_place(lists))
+
+
+def count_cost(boxes, depth, kinds, columns):
+    return pl.CostEstimate(
+        flops=8 * boxes * depth * kinds * columns,
+        bytes_accessed=boxes * kinds * columns * 2,
+        transcendentals=0,
+    )
+
+
+def count_kernel(levels, kinds, columns, *refs):
+    out_ref = refs[-1]
     done = 0
-    for level, (first, width, by_box) in enumerate(levels):
-        pair = slice(2 * level, 2 * level + 2)
-        for ref, rows in zip(lists[pair], scratch[pair]):
-            if by_box:
-                rows[...] = jnp.full(rows.shape, -1, jnp.float32)
-                rows[:, : ref.shape[1]] = ref[first : first + width, :].astype(jnp.float32)
-                continue
-            length, total = ref.shape
-            whole = length // 8 * 8
-            begin = first // LANES * LANES
-            span = min(rows.shape[0], total - begin)
-            lanes = slice(begin, begin + span)
-            pad = jnp.full((depth - length, span), -1, jnp.int32)
-            entries = jnp.concatenate([ref[:whole, lanes], ref[whole:, lanes], pad], 0)
-            rows[...] = entries.astype(jnp.float32).T
-        source_rows, kind_rows = scratch[pair]
-        offset = 0 if by_box else first % LANES
-
-        def one_box(box, _):
-            source_hot = hot(source_rows, box + offset, columns)
-            kind_hot = hot(kind_rows, box + offset, kinds)
-            counted = lax.dot_general(
-                kind_hot, source_hot, (((1,), (1,)), ((), ())), preferred_element_type=jnp.float32
-            )
-            start = pl.multiple_of((box + done) * kinds, kinds)
-            out_ref[pl.ds(start, kinds), :] = counted.astype(half)
-            return 0
-
-        lax.fori_loop(0, width, one_box, 0, unroll=min(width, 64))
+    for level, (first, width) in enumerate(levels):
+        rows = refs[2 * level : 2 * level + 2]
+        count_boxes(*rows, first, width, kinds, columns, out_ref, done)
         done += width
 
 
-def count_entries(lists, length, levels, kinds, columns, after=()):
-    depth = round_up(length, LANES)
-    boxes = sum(width for _, width, _ in levels)
-    scratch = []
-    for first, width, by_box in levels:
-        span = width if by_box else round_up(first % LANES + width, LANES)
-        scratch += [pltpu.VMEM((span, depth), jnp.float32)] * 2
+def count_entries(rows, levels, kinds, columns, after=()):
+    boxes = sum(width for _, width in levels)
     return pl.pallas_call(
         functools.partial(count_kernel, levels, kinds, columns),
         out_shape=jax.ShapeDtypeStruct((boxes * kinds, columns), jnp.bfloat16),
-        in_specs=[VMEM] * (len(lists) + len(after)),
+        in_specs=[VMEM] * (len(rows) + len(after)),
         out_specs=VMEM,
-        scratch_shapes=scratch,
         compiler_params=pltpu.CompilerParams(vmem_limit_bytes=8 << 20),
-        cost_estimate=pl.CostEstimate(
-            flops=2 * boxes * depth * kinds * columns * 4,
-            bytes_accessed=boxes * kinds * columns * 2,
-            transcendentals=0,
-        ),
+        cost_estimate=count_cost(boxes, rows[0].shape[1], kinds, columns),
         name="counts",
-    )(*lists, *after)
+    )(*rows, *after)
 
 
 def local_kernel(widths, firsts, kinds, member_ref, *refs):
@@ -292,7 +314,7 @@
     index = member.astype(jnp.int32).reshape(1)
 
     lists = (fine_source, fine_operator, parent_source.T, parent_operator.T)
-    special = group == 2 and widths[0] % (2 * LANES) == 0 and widths[1] % WINDOW == 0
+    special = group == 2 and widths[0] % (8 * WINDOW) == 0 and widths[1] % WINDOW == 0
 
     def share(whose):
         fine_size, parent_size = max(widths[0], WINDOW), max(widths[1], WINDOW)
@@ -309,32 +331,33 @@
     columns = 5 * WINDOW
     length = fine_source.shape[0]
     if special:
-        mine, theirs, *lists = pack(index, fine_parts, parent_parts, lists, widths)
+        mine, theirs = pack(index, fine_parts, parent_parts, widths)
         early = widths[0] // 2
         late = widths[0] - early
-        counted_late = ((early, late, False), (0, widths[1], True))
+        firsts = (0, early)
         summed = mine.astype(jnp.float32) + rotate(theirs, "batch", 1).astype(jnp.float32)
         own = summed.astype(jnp.bfloat16)
-        counted = [
-            count_entries(lists[:2], length, ((0, early, False),), kinds, columns),
-            count_entries(lists, length, counted_late, kinds, columns, (own,)),
-        ]
-        firsts = (0, early)
+        counted, *rows = first_counts(index, lists, widths, early, kinds, columns)
+        levels = ((early, late), (0, widths[1]))
+        counted = [counted, count_entries(rows, levels, kinds, columns, (own,))]
     else:
         summed = share(member).astype(jnp.float32)
         for step in range(1, group):
             summed += rotate(share((member + step) % group), "batch", step).astype(jnp.float32)
         own = summed.astype(jnp.bfloat16)
-        levels = ((0, widths[0], True), (0, widths[1], True))
-        lists = [
-            lax.dynamic_slice_in_dim(each, member * width, width, 0)
-            for each, width in zip(
-                (fine_source.T, fine_operator.T, *lists[2:]), (*widths[:1] * 2, *widths[1:] * 2)
-            )
-        ]
-        counted = [count_entries(lists, length, levels, kinds, columns)]
+        depth = round_up(length, LANES)
+        rows = []
+        for each, width in zip(
+            (fine_source.T, fine_operator.T, *lists[2:]), (*widths[:1] * 2, *widths[1:] * 2)
+        ):
+            each = lax.dynamic_slice_in_dim(each, member * width, width, 0).astype(jnp.float32)
+            rows.append(jnp.pad(each, ((0, 0), (0, depth - length)), constant_values=-1))
+        levels = ((0, widths[0]), (0, widths[1]))
+        counted = [count_entries(rows, levels, kinds, columns)]
         firsts = (0,)
-    blocks = [own] + [partner(own, "space", bit) for bit in range(4)]
+    blocks = [own]
+    for bit in range(4):
+        blocks.append(partner(own, "space", bit))
     local = local_of(
         index,
         counted,
@@ -372,6 +395,7 @@
         P("space", "batch", None),
         P("batch", "space"),
     )
+
     return jax.shard_map(
         body, mesh=mesh, in_specs=placed, out_specs=P("batch", "space"), check_vma=False
     )

time: 27.2 us -> 27 us (level)
  Pallas kernels: 11.3 us -> 12 us
  starting transfers between devices: 10.9 us -> 10.4 us
  waiting for transfers between devices: 4.66 us -> 4.24 us
    pallas_call x1 -> x2, Pallas kernels: 1.2 us -> 3.76 us  [the longest x1 2.84 us: first_counts(): pl.pallas_call(functools.partial(first_kernel, early, kinds, columns), ou...]
    pallas_call x2 -> x1, Pallas kernels: 3.91 us -> 2.05 us  [count_entries(): pl.pallas_call(functools.partial(count_kernel, levels, kinds, columns), o...]
    ppermute x2, waiting for transfers between devices: 2.9 us -> 2.33 us  [rotate(): lax.ppermute(value, axis, [(i, (i + step) % size) for i in range(size)])]
    ppermute x4, starting transfers between devices: 6.29 us -> 5.79 us  [partner(): lax.ppermute(value, axis, [(i, i ^ 1 << apart) for i in range(lax.axis_si...]
  transfers between devices with their start and end apart: 6 -> 6, of which waited for: 3 -> 2; matrix products, arithmetic and copies ran while one was open for 0% -> 0% of each run, Pallas kernels for 16% -> 20%
where the time goes in v3:
time: 27 us; the launch traced here: 26.8 us
  Pallas kernels  12 us (44%)
  starting transfers between devices  10.4 us (39%)
  waiting for transfers between devices  4.24 us (16%)
    ppermute x4, starting transfers between devices, partner(): lax.ppermute(value, axis, [(i, i ^ 1 << apart) for i in range(lax.axis_si...  5.79 us
    pallas_call x1, Pallas kernels, local_of(): pl.pallas_call(functools.partial(local_kernel, widths, firsts, kinds), ou...  4.7 us
    ppermute x2, starting transfers between devices, rotate(): lax.ppermute(value, axis, [(i, (i + step) % size) for i in range(size)])  4.62 us
    pallas_call x1, Pallas kernels, first_counts(): pl.pallas_call(functools.partial(first_kernel, early, kinds, columns), ou...  2.84 us
    ppermute x2, waiting for transfers between devices, rotate(): lax.ppermute(value, axis, [(i, (i + step) % size) for i in range(size)])  2.33 us
    pallas_call x1, Pallas kernels, count_entries(): pl.pallas_call(functools.partial(count_kernel, levels, kinds, columns), o...  2.05 us
    ppermute x4, waiting for transfers between devices, partner(): lax.ppermute(value, axis, [(i, i ^ 1 << apart) for i in range(lax.axis_si...  1.91 us
    pallas_call x2, Pallas kernels, evaluate(): pl.pallas_call(kernel, out_shape=jax.ShapeDtypeStruct((slots, columns), j...  1.48 us
  transfers between devices with their start and end apart: 6, of which 2 were waited for; matrix products, arithmetic and copies ran while one was open for 0% of the time, Pallas kernels for 20%

profile of v3, /device:TPU:0, one launch (start us, length us, event | category | flops | bytes accessed | tf_op | source)
XLA Modules:
  0.0 26.8 jit_solution(17132527874586627901)
XLA Ops:
  0.0 0.9 %pack.1 = (bf16[288,128]{1,0:T(8,128)(2,1)S(1)}, bf16[288,128]{1,0:T(8,128)(2,1)S(1)}) custom-call(s32[1]{0:T(128)} %bitcast.member_ref, bf16[1,512,128]{2,1,0:T(8,128)(2,1)} %fine_ref.1, bf16[1,64,128]{2,1,0:T(8,128)(2,1)} %parent_ref.1), custom_call_target="tpu_custom_call" | custom-call | tf_op jit(solution)/shard_map/pack/pallas_call | solution.py:53
  0.9 3.1 %collective-permute-start = (bf16[288,128]{1,0:T(8,128)(2,1)S(1)}, bf16[288,128]{1,0:T(8,128)(2,1)S(1)}, u32[]{:S(2)}, u32[]{:S(2)}) collective-permute-start(bf16[288,128]{1,0:T(8,128)(2,1)S(1)} %get-tuple-element.18), channel_id=1, source_target_pairs={{0,1},{1,0},{2,3},{3,2},{4,5},{5,4},{6,7},{7,6},{8,9},{9,8},{10,11... | collective-permute-start | bytes 221192 | tf_op jit(solution)/shard_map/ppermute | solution.py:25
  4.0 2.8 %first_counts.1 = (bf16[8192,160]{1,0:T(8,128)(2,1)S(1)}, f32[256,256]{1,0:T(8,128)S(1)}, f32[256,256]{1,0:T(8,128)S(1)}, f32[32,256]{1,0:T(8,128)S(1)}, f32[32,256]{1,0:T(8,128)S(1)}) custom-call(s32[1]{0:T(128)} %bitcast.member_ref, s32[189,512]{1,0:T(8,128)} %refs_0_.1, s32[189,512]{1,0:T(8,128)} %refs_1_.1, s32[64,189]{1,0:T(8,128)} %bitcast.5, ...), custom_call_target="tpu_custom_call" | custom-call | flops 2684354560 | bytes 2621440 | tf_op jit(solution)/shard_map/first_counts/pallas_call | solution.py:124
  6.8 0.0 collective-permute-done
  6.9 0.1 collective-permute-start.1
  7.0 1.6 %collective-permute-start.2 = (bf16[288,128]{1,0:T(8,128)(2,1)S(1)}, bf16[288,128]{1,0:T(8,128)(2,1)S(1)}, u32[]{:S(2)}, u32[]{:S(2)}) collective-permute-start(bf16[288,128]{1,0:T(8,128)(2,1)S(1)} %add_convert_fusion.refs_4_.refs_2_), channel_id=1, source_target_pairs={{0,4},{2,6},{4,0},{6,2},{8,12},{10,14},{12,8},{14,10},{16,20},{18,... | collective-permute-start | bytes 221192 | tf_op jit(solution)/shard_map/ppermute | solution.py:29
  8.5 1.6 %collective-permute-start.3 = (bf16[288,128]{1,0:T(8,128)(2,1)S(1)}, bf16[288,128]{1,0:T(8,128)(2,1)S(1)}, u32[]{:S(2)}, u32[]{:S(2)}) collective-permute-start(bf16[288,128]{1,0:T(8,128)(2,1)S(1)} %add_convert_fusion.refs_4_.refs_2_), channel_id=1, source_target_pairs={{0,8},{2,10},{4,12},{6,14},{8,0},{10,2},{12,4},{14,6},{16,24},{18,... | collective-permute-start | bytes 221192 | tf_op jit(solution)/shard_map/ppermute | solution.py:29
  10.1 2.6 %collective-permute-start.4 = (bf16[288,128]{1,0:T(8,128)(2,1)S(1)}, bf16[288,128]{1,0:T(8,128)(2,1)S(1)}, u32[]{:S(2)}, u32[]{:S(2)}) collective-permute-start(bf16[288,128]{1,0:T(8,128)(2,1)S(1)} %add_convert_fusion.refs_4_.refs_2_), channel_id=1, source_target_pairs={{0,16},{2,18},{4,20},{6,22},{8,24},{10,26},{12,28},{14,30},{16,0},... | collective-permute-start | bytes 221192 | tf_op jit(solution)/shard_map/ppermute | solution.py:29
  12.7 0.0 copy-start.2
  12.7 0.0 copy-start.3
  12.7 0.0 copy-start.4
  12.7 2.0 %counts.1.refs_1_ = bf16[10240,160]{1,0:T(8,128)(2,1)S(1)} custom-call(f32[256,256]{1,0:T(8,128)S(1)} %get-tuple-element.13.refs_0_, f32[256,256]{1,0:T(8,128)S(1)} %get-tuple-element.14.refs_1_, f32[32,256]{1,0:T(8,128)S(1)} %get-tuple-element.15.refs_2_, f32[32,256]{1,0:T(8,128)S(1)} %get-tuple-element.16.refs_3_, ...), custom_call_target="tpu_custom_call" | custom-call | flops 3355443200 | bytes 3276800 | tf_op jit(solution)/shard_map/counts/pallas_call | solution.py:155
  14.7 0.0 collective-permute-done.1.refs_3_
  14.8 0.0 collective-permute-done.2.refs_4_
  14.8 0.0 collective-permute-done.3.refs_5_
  14.8 1.9 %collective-permute-done.4.refs_6_ = bf16[288,128]{1,0:T(8,128)(2,1)S(1)} collective-permute-done((bf16[288,128]{1,0:T(8,128)(2,1)S(1)}, bf16[288,128]{1,0:T(8,128)(2,1)S(1)}, u32[]{:S(2)}, u32[]{:S(2)}) %collective-permute-start.4) | collective-permute-done | bytes 73760 | tf_op jit(solution)/shard_map/ppermute | solution.py:29
  16.7 0.0 copy-done.2
  16.7 0.0 copy-done.3
  16.7 0.0 copy-done.4
  16.7 0.0 copy-start
  16.7 0.0 copy-start.1
  16.7 4.7 %far.1.local_ref = bf16[256,128]{1,0:T(8,128)(2,1)S(1)} custom-call(s32[1]{0:T(128)} %bitcast.member_ref, bf16[8192,160]{1,0:T(8,128)(2,1)S(1)} %get-tuple-element.12.refs_0_, bf16[10240,160]{1,0:T(8,128)(2,1)S(1)} %counts.1.refs_1_, bf16[288,128]{1,0:T(8,128)(2,1)S(1)} %add_convert_fusion.refs_4_.refs_2_, ...), custom_call_target="tpu_custom_call" | custom-call | flops 4831838208 | bytes 9437184 | tf_op jit(solution)/shard_map/far/pallas_call | solution.py:219
  21.4 1.6 %collective-permute-start.5 = (bf16[256,128]{1,0:T(8,128)(2,1)S(1)}, bf16[256,128]{1,0:T(8,128)(2,1)S(1)}, u32[]{:S(2)}, u32[]{:S(2)}) collective-permute-start(bf16[256,128]{1,0:T(8,128)(2,1)S(1)} %far.1.local_ref), channel_id=1, source_target_pairs={{0,1},{1,0},{2,3},{3,2},{4,5},{5,4},{6,7},{7,6},{8,9},{9,8},{10,11... | collective-permute-start | bytes 196616 | tf_op jit(solution)/shard_map/ppermute | solution.py:25
  23.0 0.0 copy-done
  23.0 0.0 copy-done.1
  23.0 0.4 %slots.2.own_ref = f32[16,256]{1,0:T(8,128)S(1)} custom-call(s32[1]{0:T(128)} %bitcast.member_ref, bf16[256,128]{1,0:T(8,128)(2,1)S(1)} %far.1.local_ref, bf16[512,16,128]{2,1,0:T(8,128)(2,1)S(1)} %copy-done, s32[1,512]{1,0:T(1,128)S(1)} %copy-done.1), custom_call_target="tpu_custom_call" | custom-call | flops 268435456 | bytes 1048576 | tf_op jit(solution)/shard_map/slots/pallas_call | solution.py:281
  23.4 2.3 %collective-permute-done.5.local_ref = bf16[256,128]{1,0:T(8,128)(2,1)S(1)} collective-permute-done((bf16[256,128]{1,0:T(8,128)(2,1)S(1)}, bf16[256,128]{1,0:T(8,128)(2,1)S(1)}, u32[]{:S(2)}, u32[]{:S(2)}) %collective-permute-start.5) | collective-permute-done | bytes 65568 | tf_op jit(solution)/shard_map/ppermute | solution.py:25
  25.7 1.1 %slots.3 = f32[16,512]{1,0:T(8,128)} custom-call(s32[1]{0:T(128)} %bitcast.member_ref, bf16[256,128]{1,0:T(8,128)(2,1)S(1)} %collective-permute-done.5.local_ref, bf16[512,16,128]{2,1,0:T(8,128)(2,1)S(1)} %copy-done, s32[1,512]{1,0:T(1,128)S(1)} %copy-done.1, f32[16,256]{1,0:T(8,128)S(1)} %slots.2.own_ref), custom_call_target="tpu_custom_call" | custom-call | flops 268435456 | bytes 1048576 | tf_op jit(solution)/shard_map/slots/pallas_call | solution.py:281
  (1 shorter events, 0.0 us)
Async XLA Ops:
  0.9 5.9 %collective-permute-start = (bf16[288,128]{1,0:T(8,128)(2,1)S(1)}, bf16[288,128]{1,0:T(8,128)(2,1)S(1)}, u32[]{:S(2)}, u32[]{:S(2)}) collective-permute-start(bf16[288,128]{1,0:T(8,128)(2,1)S(1)} %get-tuple-element.18), channel_id=1, source_target_pairs={{0,1},{1,0},{2,3},{3,2},{4,5},{5,4},{6,7},{7,6},{8,9},{9,8},{10,11... | collective-permute-start | bytes 221192 | tf_op jit(solution)/shard_map/ppermute | solution.py:25
  6.9 7.9 %collective-permute-start.1 = (bf16[288,128]{1,0:T(8,128)(2,1)S(1)}, bf16[288,128]{1,0:T(8,128)(2,1)S(1)}, u32[]{:S(2)}, u32[]{:S(2)}) collective-permute-start(bf16[288,128]{1,0:T(8,128)(2,1)S(1)} %add_convert_fusion.refs_4_.refs_2_), channel_id=1, source_target_pairs={{0,2},{2,0},{4,6},{6,4},{8,10},{10,8},{12,14},{14,12},{16,18},{18,... | collective-permute-start | bytes 221192 | tf_op jit(solution)/shard_map/ppermute | solution.py:29
  7.0 7.8 %collective-permute-start.2 = (bf16[288,128]{1,0:T(8,128)(2,1)S(1)}, bf16[288,128]{1,0:T(8,128)(2,1)S(1)}, u32[]{:S(2)}, u32[]{:S(2)}) collective-permute-start(bf16[288,128]{1,0:T(8,128)(2,1)S(1)} %add_convert_fusion.refs_4_.refs_2_), channel_id=1, source_target_pairs={{0,4},{2,6},{4,0},{6,2},{8,12},{10,14},{12,8},{14,10},{16,20},{18,... | collective-permute-start | bytes 221192 | tf_op jit(solution)/shard_map/ppermute | solution.py:29
  8.5 6.2 %collective-permute-start.3 = (bf16[288,128]{1,0:T(8,128)(2,1)S(1)}, bf16[288,128]{1,0:T(8,128)(2,1)S(1)}, u32[]{:S(2)}, u32[]{:S(2)}) collective-permute-start(bf16[288,128]{1,0:T(8,128)(2,1)S(1)} %add_convert_fusion.refs_4_.refs_2_), channel_id=1, source_target_pairs={{0,8},{2,10},{4,12},{6,14},{8,0},{10,2},{12,4},{14,6},{16,24},{18,... | collective-permute-start | bytes 221192 | tf_op jit(solution)/shard_map/ppermute | solution.py:29
  10.1 6.6 %collective-permute-start.4 = (bf16[288,128]{1,0:T(8,128)(2,1)S(1)}, bf16[288,128]{1,0:T(8,128)(2,1)S(1)}, u32[]{:S(2)}, u32[]{:S(2)}) collective-permute-start(bf16[288,128]{1,0:T(8,128)(2,1)S(1)} %add_convert_fusion.refs_4_.refs_2_), channel_id=1, source_target_pairs={{0,16},{2,18},{4,20},{6,22},{8,24},{10,26},{12,28},{14,30},{16,0},... | collective-permute-start | bytes 221192 | tf_op jit(solution)/shard_map/ppermute | solution.py:29
  12.7 4.0 %copy-start.2 = (bf16[64,128,128]{2,1,0:T(8,128)(2,1)S(1)}, bf16[64,128,128]{2,1,0:T(8,128)(2,1)}, u32[]{:S(2)}) copy-start(bf16[64,128,128]{2,1,0:T(8,128)(2,1)} %param.18) | copy-start | bytes 6291460
  12.7 4.0 %copy-start.3 = (bf16[8,128,128]{2,1,0:T(8,128)(2,1)S(1)}, bf16[8,128,128]{2,1,0:T(8,128)(2,1)}, u32[]{:S(2)}) copy-start(bf16[8,128,128]{2,1,0:T(8,128)(2,1)} %refs_9_.1) | copy-start | bytes 786436
  12.7 4.0 %copy-start.4 = (f32[64,128]{1,0:T(8,128)S(1)}, f32[64,128]{1,0:T(8,128)}, u32[]{:S(2)}) copy-start(f32[64,128]{1,0:T(8,128)} %refs_8_.1) | copy-start | bytes 98308
  16.7 6.3 %copy-start = (bf16[512,16,128]{2,1,0:T(8,128)(2,1)S(1)}, bf16[512,16,128]{2,1,0:T(8,128)(2,1)}, u32[]{:S(2)}) copy-start(bf16[512,16,128]{2,1,0:T(8,128)(2,1)} %basis_ref.3) | copy-start | bytes 6291460
  16.7 6.3 %copy-start.1 = (s32[1,512]{1,0:T(1,128)S(1)}, s32[1,512]{1,0:T(1,128)}, u32[]{:S(2)}) copy-start(s32[1,512]{1,0:T(1,128)} %counts_ref.3) | copy-start | bytes 6148
  21.4 4.3 %collective-permute-start.5 = (bf16[256,128]{1,0:T(8,128)(2,1)S(1)}, bf16[256,128]{1,0:T(8,128)(2,1)S(1)}, u32[]{:S(2)}, u32[]{:S(2)}) collective-permute-start(bf16[256,128]{1,0:T(8,128)(2,1)S(1)} %far.1.local_ref), channel_id=1, source_target_pairs={{0,1},{1,0},{2,3},{3,2},{4,5},{5,4},{6,7},{7,6},{8,9},{9,8},{10,11... | collective-permute-start | bytes 196616 | tf_op jit(solution)/shard_map/ppermute | solution.py:25

commit v4 on v3

v4 whole, which is shorter than its diff:
```python
import functools

import jax
import jax.numpy as jnp
from jax import lax
from jax.experimental import pallas as pl
from jax.experimental.pallas import tpu as pltpu
from jax.sharding import PartitionSpec as P


NTERMS = 121
WINDOW = 32
LANES = 128
VMEM = pl.BlockSpec(memory_space=pltpu.VMEM)
HBM = pl.BlockSpec(memory_space=pltpu.HBM)
SMEM = pl.BlockSpec(memory_space=pltpu.SMEM)


def round_up(value, step):
    return -(-value // step) * step


def rotate(value, axis, step):
    size = lax.axis_size(axis)
    return lax.ppermute(value, axis, [(i, (i + step) % size) for i in range(size)])


def partner(value, axis, apart):
    return lax.ppermute(value, axis, [(i, i ^ 1 << apart) for i in range(lax.axis_size(axis))])


def pack_kernel(widths, member_ref, fine_ref, parent_ref, mine_ref, theirs_ref, sem):
    member = member_ref[0]
    fine, parent = widths
    copies = []
    for at, out in ((1 - member, theirs_ref), (member, mine_ref)):
        start = pl.multiple_of(at * fine, WINDOW)
        for source, row, width in (
            (fine_ref.at[0, pl.ds(start, fine), :], 0, fine),
            (parent_ref.at[0], fine, parent),
        ):
            target = out.at[pl.ds(row, width), :]
            copies.append(pltpu.make_async_copy(source, target, sem.at[len(copies)]))
    for copy in copies:
        copy.start()
    for copy in copies:
        copy.wait()


def in_place(values):
    return [pltpu.with_memory_space_constraint(each, pltpu.HBM) for each in values]


def pack(member, fine_parts, parent_parts, widths):
    chunk = jax.ShapeDtypeStruct((sum(widths), fine_parts.shape[2]), fine_parts.dtype)
    return pl.pallas_call(
        functools.partial(pack_kernel, widths),
        out_shape=[chunk, chunk],
        in_specs=[SMEM, HBM, HBM],
        out_specs=[VMEM, VMEM],
        scratch_shapes=[pltpu.SemaphoreType.DMA((4,))],
        compiler_params=pltpu.CompilerParams(vmem_limit_bytes=4 << 20),
        name="pack",
    )(member, *in_place((fine_parts, parent_parts)))


def count_boxes(source_rows, kind_rows, first, width, kinds, columns, out_ref):
    depth = source_rows.shape[1]
    half, quarter = jnp.bfloat16, jnp.float8_e4m3fn
    rows_iota = lax.broadcasted_iota(jnp.int32, (32, depth), 0).astype(half)
    one = jnp.ones((), quarter)
    zero = jnp.zeros((), quarter)

    def hot(row_ref, row, size):
        values = jnp.broadcast_to(row_ref[pl.ds(row, 1), :], (32, depth)).astype(half)
        pieces = [jnp.where(values == rows_iota + 32 * k, one, zero) for k in range(size // 32)]
        return jnp.concatenate(pieces, 0)

    def one_box(box, _):
        source_hot = hot(source_rows, box + first, columns)
        kind_hot = hot(kind_rows, box + first, kinds)
        counted = lax.dot_general(
            kind_hot, source_hot, (((1,), (1,)), ((), ())), preferred_element_type=jnp.float32
        )
        start = pl.multiple_of(box * kinds, kinds)
        out_ref[pl.ds(start, kinds), :] = counted.astype(half)
        return 0

    lax.fori_loop(0, width, one_box, 0, unroll=min(width, 64))


def first_kernel(early, kinds, columns, member_ref, *refs):
    lists, out_ref, rows, loaded, sem = refs[:4], refs[4], refs[5:9], refs[9:13], refs[13]
    member = member_ref[0]
    length, fine = loaded[0].shape
    lanes = pl.ds(pl.multiple_of(member * fine, LANES), fine)
    sources = [ref.at[:, lanes] for ref in lists[:2]] + list(lists[2:])
    copies = [
        pltpu.make_async_copy(ref, out, sem.at[i]) for i, (ref, out) in enumerate(zip(sources, loaded))
    ]
    for copy in copies:
        copy.start()
    depth = rows[0].shape[1]
    whole = length // 8 * 8
    pad = jnp.full((depth - length, fine), -1, jnp.int32)
    for copy, ref, out in zip(copies[:2], loaded[:2], rows[:2]):
        copy.wait()
        entries = jnp.concatenate([ref[:whole, :], ref[whole:, :], pad], 0)
        out[...] = entries.astype(jnp.float32).T
    for copy, ref, out in zip(copies[2:], loaded[2:], rows[2:]):
        copy.wait()
        out[...] = jnp.full(out.shape, -1, jnp.float32)
        out[:, :length] = ref[...].astype(jnp.float32)
    count_boxes(*rows[:2], 0, early, kinds, columns, out_ref)


def first_counts(member, lists, widths, early, kinds, columns):
    length = lists[0].shape[0]
    depth = round_up(length, LANES)
    rows = [jax.ShapeDtypeStruct((width, depth), jnp.float32) for width in widths for _ in "ab"]
    loaded = [pltpu.VMEM((length, widths[0]), jnp.int32)] * 2
    loaded += [pltpu.VMEM((widths[1], length), jnp.int32)] * 2
    return pl.pallas_call(
        functools.partial(first_kernel, early, kinds, columns),
        out_shape=[jax.ShapeDtypeStruct((early * kinds, columns), jnp.bfloat16)] + rows,
        in_specs=[SMEM] + [HBM] * 4,
        out_specs=[VMEM] * 5,
        scratch_shapes=loaded + [pltpu.SemaphoreType.DMA((4,))],
        compiler_params=pltpu.CompilerParams(vmem_limit_bytes=8 << 20),
        cost_estimate=count_cost(early, depth, kinds, columns),
        name="first_counts",
    )(member, *in_place(lists))


def count_cost(boxes, depth, kinds, columns):
    return pl.CostEstimate(
        flops=8 * boxes * depth * kinds * columns,
        bytes_accessed=boxes * kinds * columns * 2,
        transcendentals=0,
    )


def count_kernel(levels, kinds, columns, *refs):
    for level, (first, width) in enumerate(levels):
        rows = refs[2 * level : 2 * level + 2]
        out_ref = refs[level - len(levels)]
        count_boxes(*rows, first, width, kinds, columns, out_ref)


def count_entries(rows, levels, kinds, columns, after=()):
    boxes = [width for _, width in levels]
    return pl.pallas_call(
        functools.partial(count_kernel, levels, kinds, columns),
        out_shape=[jax.ShapeDtypeStruct((each * kinds, columns), jnp.bfloat16) for each in boxes],
        in_specs=[VMEM] * (len(rows) + len(after)),
        out_specs=[VMEM] * len(boxes),
        compiler_params=pltpu.CompilerParams(vmem_limit_bytes=8 << 20),
        cost_estimate=count_cost(sum(boxes), rows[0].shape[1], kinds, columns),
        name="counts",
    )(*rows, *after)


def contract(counted, firsts, blocks, begin, kinds, ops_ref, grouped, total):
    boxes, coef = total.shape
    pitch = grouped.shape[0] // boxes
    for start in range(0, boxes, WINDOW):
        count = min(WINDOW, boxes - start)
        at = begin + start
        nearby = jnp.concatenate([ref[at : at + WINDOW, :] for ref in blocks], 0)
        which = max(i for i in range(len(firsts)) if firsts[i] <= start)
        at = (start - firsts[which]) * kinds
        values = jnp.dot(
            counted[which][at : at + count * kinds, :], nearby, preferred_element_type=jnp.float32
        )
        for box in range(count):
            row = (start + box) * pitch
            grouped[row : row + kinds, :] = values[box * kinds : (box + 1) * kinds]

    step = 8
    for at in range(0, kinds, step):
        picked = [
            grouped[pl.ds(at + k, boxes, stride=pitch), :].astype(jnp.bfloat16)
            for k in range(step)
        ]
        term = jnp.dot(
            jnp.concatenate(picked, 1),
            ops_ref[at * coef : (at + step) * coef, :],
            preferred_element_type=jnp.float32,
        )
        total[...] = term + total[...] if at else term


def contract_scratch(boxes, kinds, coef):
    return [pltpu.VMEM((boxes * (kinds + 4), coef), jnp.float32), pltpu.VMEM((boxes, coef), jnp.float32)]


def far_kernel(firsts, kinds, *refs):
    counted, blocks = refs[: len(firsts)], refs[len(firsts) : len(firsts) + 5]
    ops_ref, out_ref, grouped, total = refs[len(firsts) + 5 :]
    contract(counted, firsts, blocks, 0, kinds, ops_ref, grouped, total)
    out_ref[...] = total[...].astype(out_ref.dtype)


def far_of(counted, firsts, blocks, flat_ops, boxes, kinds):
    coef = flat_ops.shape[1]
    return pl.pallas_call(
        functools.partial(far_kernel, firsts, kinds),
        out_shape=jax.ShapeDtypeStruct((boxes, coef), jnp.bfloat16),
        in_specs=[VMEM] * (6 + len(counted)),
        out_specs=VMEM,
        scratch_shapes=contract_scratch(boxes, kinds, coef),
        compiler_params=pltpu.CompilerParams(vmem_limit_bytes=24 << 20),
        cost_estimate=pl.CostEstimate(
            flops=8 * boxes * kinds * coef * 256,
            bytes_accessed=boxes * kinds * coef * 4,
            transcendentals=0,
        ),
        name="far",
    )(*counted, *blocks, flat_ops)


def slots_of(basis_ref, counts_ref, box, local):
    count, coef = local.shape
    slots = basis_ref.shape[1]
    pairs = count // 2
    odd = lax.broadcasted_iota(jnp.int32, local.shape, 0) % 2
    zero = jnp.zeros_like(local)
    right = jnp.concatenate(
        [jnp.where(odd == 0, local, zero), jnp.where(odd == 1, local, zero)], 1
    )
    left = basis_ref[pl.ds(box, count)].reshape(pairs, 2, slots, coef)
    left = jnp.concatenate([left[:, 0], left[:, 1]], 2).reshape(pairs * slots, 2 * coef)
    values = lax.dot_general(
        left, right, (((1,), (1,)), ((), ())), preferred_element_type=jnp.float32
    ).reshape(pairs, slots, count)
    lane = lax.broadcasted_iota(jnp.int32, (slots, count), 1) // 2
    summed = jnp.zeros((slots, count), jnp.float32)
    for pair in range(pairs):
        summed += jnp.where(lane == pair, values[pair], 0.0)
    slot = lax.broadcasted_iota(jnp.int32, summed.shape, 0)
    limit = counts_ref[:, pl.ds(box, count)]
    return jnp.where(slot < limit, summed, 0.0)


def evaluate(far, moved, basis_ref, counts_ref, first):
    whole = moved + far.astype(jnp.float32)
    keep = lax.broadcasted_iota(jnp.int32, whole.shape, 1) < NTERMS
    local = jnp.where(keep, whole, 0.0).astype(jnp.bfloat16)
    width = local.shape[0]
    pieces = []
    for piece in range(0, width, LANES):
        box = pl.multiple_of(first + piece, LANES)
        pieces.append(slots_of(basis_ref, counts_ref, box, local[piece : piece + LANES]))
    return jnp.concatenate(pieces, 1)


def own_kernel(kinds, fine, member_ref, count_ref, *refs):
    blocks = refs[:5]
    (ops_ref, coarse_ref, shift_ref, far_ref, basis_ref, counts_ref) = refs[5:11]
    out_ref, rest_ref, grouped, total, moved = refs[11:]
    contract((count_ref,), (0,), blocks, fine, kinds, ops_ref, grouped, total)
    parent_local = (coarse_ref[...] + total[...]).astype(jnp.bfloat16)
    parents = parent_local.shape[0]
    octants = shift_ref.shape[0]
    for octant in range(octants):
        moved[pl.ds(octant, parents, stride=octants), :] = jnp.dot(
            parent_local, shift_ref[octant], preferred_element_type=jnp.float32
        )
    width = far_ref.shape[0]
    first = pl.multiple_of(member_ref[0] * width, LANES)
    out_ref[...] = evaluate(
        far_ref[...], moved[pl.ds(first, width), :], basis_ref, counts_ref, first
    )
    rest = rest_ref.shape[0]
    rest_ref[...] = moved[pl.ds(pl.multiple_of((1 - member_ref[0]) * rest, LANES), rest), :]


def own_of(member, counted, blocks, fine, flat_ops, coarse, shift, far, basis, counts, kinds, rest):
    slots, coef = basis.shape[1:]
    parents = coarse.shape[0]
    return pl.pallas_call(
        functools.partial(own_kernel, kinds, fine),
        out_shape=[
            jax.ShapeDtypeStruct((slots, far.shape[0]), jnp.float32),
            jax.ShapeDtypeStruct((rest, coef), jnp.float32),
        ],
        in_specs=[SMEM] + [VMEM] * 12,
        out_specs=[VMEM, VMEM],
        scratch_shapes=contract_scratch(parents, kinds, coef)
        + [pltpu.VMEM((parents * shift.shape[0], coef), jnp.float32)],
        compiler_params=pltpu.CompilerParams(vmem_limit_bytes=16 << 20),
        cost_estimate=pl.CostEstimate(
            flops=8 * parents * kinds * coef * 256,
            bytes_accessed=parents * kinds * coef * 4,
            transcendentals=0,
        ),
        name="own",
    )(member, counted, *blocks, flat_ops, coarse, shift, far, basis, counts)


def other_kernel(member_ref, far_ref, moved_ref, basis_ref, counts_ref, own_ref, out_ref):
    width = far_ref.shape[0]
    out_ref[:, pl.ds(pl.multiple_of(member_ref[0] * width, LANES), width)] = own_ref[...]
    first = pl.multiple_of((1 - member_ref[0]) * width, LANES)
    out_ref[:, pl.ds(first, width)] = evaluate(
        far_ref[...], moved_ref[...], basis_ref, counts_ref, first
    )


def other_of(member, far, moved, basis, counts, own):
    slots = basis.shape[1]
    return pl.pallas_call(
        other_kernel,
        out_shape=jax.ShapeDtypeStruct((slots, basis.shape[0]), jnp.float32),
        in_specs=[SMEM] + [VMEM] * 5,
        out_specs=VMEM,
        compiler_params=pltpu.CompilerParams(vmem_limit_bytes=16 << 20),
        cost_estimate=pl.CostEstimate(
            flops=2 * far.shape[0] * slots * 256 * 128,
            bytes_accessed=far.shape[0] * slots * 256,
            transcendentals=0,
        ),
        name="other",
    )(member, far, moved, basis, counts, own)


def body(
    fine_parts,
    parent_parts,
    coarse_local,
    fine_source,
    fine_operator,
    parent_source,
    parent_operator,
    operators,
    child_shift,
    basis,
    counts,
):
    group = lax.axis_size("batch")
    member = lax.axis_index("batch")
    kinds, coef, _ = operators.shape
    fine_total, parent_total = fine_source.shape[1], parent_source.shape[1]
    fine = fine_total // group
    widths = (fine, parent_total)
    index = member.astype(jnp.int32).reshape(1)
    lists = (fine_source, fine_operator, parent_source.T, parent_operator.T)
    special = group == 2 and fine % (8 * WINDOW) == 0

    def share(whose):
        fine_at = whose * fine // WINDOW * WINDOW
        mine = lax.dynamic_slice_in_dim(fine_parts[0], fine_at, max(fine, WINDOW), 0)
        return jnp.concatenate([mine, parent_parts[0]], 0)

    columns = 5 * WINDOW
    length = fine_source.shape[0]
    if special:
        mine, theirs = pack(index, fine_parts, parent_parts, widths)
        early = fine // 2
        summed = mine.astype(jnp.float32) + rotate(theirs, "batch", 1).astype(jnp.float32)
        own = summed.astype(jnp.bfloat16)
        counted, *rows = first_counts(index, lists, widths, early, kinds, columns)
        levels = ((early, fine - early), (0, parent_total))
        late, parent_counted = count_entries(rows, levels, kinds, columns, (own,))
        counted = [counted, late]
        firsts = (0, early)
    else:
        summed = share(member).astype(jnp.float32)
        for step in range(1, group):
            summed += rotate(share((member + step) % group), "batch", step).astype(jnp.float32)
        own = summed.astype(jnp.bfloat16)
        fine_lists = [
            lax.dynamic_slice_in_dim(each.T, member * fine, fine, 0) for each in lists[:2]
        ]
        rows = [
            jnp.pad(
                each.astype(jnp.float32),
                ((0, 0), (0, round_up(length, LANES) - length)),
                constant_values=-1,
            )
            for each in (*fine_lists, *lists[2:])
        ]
        *counted, parent_counted = count_entries(
            rows, ((0, fine), (0, parent_total)), kinds, columns
        )
        firsts = (0,)
    blocks = [own]
    for bit in range(4):
        blocks.append(partner(own, "space", bit))
    flat_ops = operators.reshape(kinds * coef, coef)
    far = far_of(counted, firsts, blocks, flat_ops, fine, kinds)
    fine_rows = max(fine, WINDOW)
    parent_side = (parent_counted, blocks, fine_rows, flat_ops, coarse_local, child_shift)
    if special:
        other = rotate(far, "batch", 1)
        mine, moved = own_of(index, *parent_side, far, basis, counts, kinds, fine)
        return other_of(index, other, moved, basis, counts, mine)
    gathered = jnp.zeros((fine_total, coef), far.dtype)
    for step in range(group):
        piece = rotate(far, "batch", step) if step else far
        at = (member - step) % group * fine
        gathered = lax.dynamic_update_slice_in_dim(gathered, piece, at, 0)
    values, _ = own_of(index * 0, *parent_side, gathered, basis, counts, kinds, LANES)
    return values


def solution(mesh):
    placed = (
        P("batch", "space", None),
        P("batch", "space", None),
        P("space", None),
        P(None, "space"),
        P(None, "space"),
        P(None, "space"),
        P(None, "space"),
        P(),
        P(),
        P("space", "batch", None),
        P("batch", "space"),
    )

    return jax.shard_map(
        body, mesh=mesh, in_specs=placed, out_specs=P("batch", "space"), check_vma=False
    )
```

time: 27 us -> 26.2 us (0.970)
  waiting for transfers between devices: 4.24 us -> 2.93 us
  Pallas kernels: 12 us -> 12.4 us
    ppermute x2, waiting for transfers between devices: 2.33 us -> 1.01 us  [rotate(): lax.ppermute(value, axis, [(i, (i + step) % size) for i in range(size)])]
    pallas_call x1, Pallas kernels: 2.05 us -> 2.38 us  [count_entries(): pl.pallas_call(functools.partial(count_kernel, levels, kinds, columns), o...]
  transfers between devices with their start and end apart: 6 -> 6, of which waited for: 2 -> 2; matrix products, arithmetic and copies ran while one was open for 0% -> 0% of each run, Pallas kernels for 20% -> 27%
where the time goes in v4:
time: 26.2 us; the launch traced here: 26 us
  Pallas kernels  12.4 us (47%)
  starting transfers between devices  10.5 us (40%)
  waiting for transfers between devices  2.93 us (11%)
    ppermute x4, starting transfers between devices, partner(): lax.ppermute(value, axis, [(i, i ^ 1 << apart) for i in range(lax.axis_si...  5.85 us
    ppermute x2, starting transfers between devices, rotate(): lax.ppermute(value, axis, [(i, (i + step) % size) for i in range(size)])  4.65 us
    pallas_call x1, Pallas kernels, far_of(): pl.pallas_call(functools.partial(far_kernel, firsts, kinds), out_shape=ja...  3.52 us
    pallas_call x1, Pallas kernels, first_counts(): pl.pallas_call(functools.partial(first_kernel, early, kinds, columns), ou...  2.84 us
    pallas_call x1, Pallas kernels, count_entries(): pl.pallas_call(functools.partial(count_kernel, levels, kinds, columns), o...  2.38 us
    ppermute x4, waiting for transfers between devices, partner(): lax.ppermute(value, axis, [(i, i ^ 1 << apart) for i in range(lax.axis_si...  1.92 us
    pallas_call x1, Pallas kernels, own_of(): pl.pallas_call(functools.partial(own_kernel, kinds, fine), out_shape=[jax...  1.72 us
    pallas_call x1, Pallas kernels, other_of(): pl.pallas_call(other_kernel, out_shape=jax.ShapeDtypeStruct((slots, basis...  1.05 us
  transfers between devices with their start and end apart: 6, of which 2 were waited for; matrix products, arithmetic and copies ran while one was open for 0% of the time, Pallas kernels for 27%

profile of v4, /device:TPU:0, one launch (start us, length us, event | category | flops | bytes accessed | tf_op | source)
XLA Modules:
  0.0 26.0 jit_solution(8856150285650390051)
XLA Ops:
  0.0 0.9 %pack.1 = (bf16[320,128]{1,0:T(8,128)(2,1)S(1)}, bf16[320,128]{1,0:T(8,128)(2,1)S(1)}) custom-call(s32[1]{0:T(128)} %bitcast.member_ref, bf16[1,512,128]{2,1,0:T(8,128)(2,1)} %fine_ref.1, bf16[1,64,128]{2,1,0:T(8,128)(2,1)} %parent_ref.1), custom_call_target="tpu_custom_call" | custom-call | tf_op jit(solution)/shard_map/pack/pallas_call | solution.py:56
  0.9 3.1 %collective-permute-start = (bf16[320,128]{1,0:T(8,128)(2,1)S(1)}, bf16[320,128]{1,0:T(8,128)(2,1)S(1)}, u32[]{:S(2)}, u32[]{:S(2)}) collective-permute-start(bf16[320,128]{1,0:T(8,128)(2,1)S(1)} %get-tuple-element.22), channel_id=1, source_target_pairs={{0,1},{1,0},{2,3},{3,2},{4,5},{5,4},{6,7},{7,6},{8,9},{9,8},{10,11... | collective-permute-start | bytes 245768 | tf_op jit(solution)/shard_map/ppermute | solution.py:25
  4.0 2.8 %first_counts.1 = (bf16[8192,160]{1,0:T(8,128)(2,1)S(1)}, f32[256,256]{1,0:T(8,128)S(1)}, f32[256,256]{1,0:T(8,128)S(1)}, f32[64,256]{1,0:T(8,128)S(1)}, f32[64,256]{1,0:T(8,128)S(1)}) custom-call(s32[1]{0:T(128)} %bitcast.member_ref, s32[189,512]{1,0:T(8,128)} %refs_0_.1, s32[189,512]{1,0:T(8,128)} %refs_1_.1, s32[64,189]{1,0:T(8,128)} %bitcast.6, ...), custom_call_target="tpu_custom_call" | custom-call | flops 2684354560 | bytes 2621440 | tf_op jit(solution)/shard_map/first_counts/pallas_call | solution.py:123
  6.8 0.0 collective-permute-done
  6.9 0.1 collective-permute-start.1
  7.0 1.6 %collective-permute-start.2 = (bf16[320,128]{1,0:T(8,128)(2,1)S(1)}, bf16[320,128]{1,0:T(8,128)(2,1)S(1)}, u32[]{:S(2)}, u32[]{:S(2)}) collective-permute-start(bf16[320,128]{1,0:T(8,128)(2,1)S(1)} %add_convert_fusion.refs_4_.refs_2_.refs_0_), channel_id=1, source_target_pairs={{0,4},{2,6},{4,0},{6,2},{8,12},{10,14},{12,8},{14,10},{16,20},{18,... | collective-permute-start | bytes 245768 | tf_op jit(solution)/shard_map/ppermute | solution.py:29
  8.6 1.6 %collective-permute-start.3 = (bf16[320,128]{1,0:T(8,128)(2,1)S(1)}, bf16[320,128]{1,0:T(8,128)(2,1)S(1)}, u32[]{:S(2)}, u32[]{:S(2)}) collective-permute-start(bf16[320,128]{1,0:T(8,128)(2,1)S(1)} %add_convert_fusion.refs_4_.refs_2_.refs_0_), channel_id=1, source_target_pairs={{0,8},{2,10},{4,12},{6,14},{8,0},{10,2},{12,4},{14,6},{16,24},{18,... | collective-permute-start | bytes 245768 | tf_op jit(solution)/shard_map/ppermute | solution.py:29
  10.2 2.6 %collective-permute-start.4 = (bf16[320,128]{1,0:T(8,128)(2,1)S(1)}, bf16[320,128]{1,0:T(8,128)(2,1)S(1)}, u32[]{:S(2)}, u32[]{:S(2)}) collective-permute-start(bf16[320,128]{1,0:T(8,128)(2,1)S(1)} %add_convert_fusion.refs_4_.refs_2_.refs_0_), channel_id=1, source_target_pairs={{0,16},{2,18},{4,20},{6,22},{8,24},{10,26},{12,28},{14,30},{16,0},... | collective-permute-start | bytes 245768 | tf_op jit(solution)/shard_map/ppermute | solution.py:29
  12.7 0.0 copy-start.1
  12.7 2.4 %counts.1 = (bf16[8192,160]{1,0:T(8,128)(2,1)S(1)}, bf16[4096,160]{1,0:T(8,128)(2,1)S(1)}) custom-call(f32[256,256]{1,0:T(8,128)S(1)} %get-tuple-element.17.refs_0_, f32[256,256]{1,0:T(8,128)S(1)} %get-tuple-element.18.refs_1_, f32[64,256]{1,0:T(8,128)S(1)} %get-tuple-element.19.refs_2_, f32[64,256]{1,0:T(8,128)S(1)} %get-tuple-element.20.refs_3_, ...), custom_call_target="tpu_custom_call" | custom-call | flops 4026531840 | bytes 3932160 | tf_op jit(solution)/shard_map/counts/pallas_call | solution.py:152
  15.1 0.0 collective-permute-done.1.refs_3_.refs_1_
  15.1 0.0 collective-permute-done.2.refs_4_.refs_2_
  15.2 0.0 collective-permute-done.3.refs_5_.refs_3_
  15.2 1.9 %collective-permute-done.4.refs_6_.refs_4_ = bf16[320,128]{1,0:T(8,128)(2,1)S(1)} collective-permute-done((bf16[320,128]{1,0:T(8,128)(2,1)S(1)}, bf16[320,128]{1,0:T(8,128)(2,1)S(1)}, u32[]{:S(2)}, u32[]{:S(2)}) %collective-permute-start.4) | collective-permute-done | bytes 81952 | tf_op jit(solution)/shard_map/ppermute | solution.py:29
  17.1 0.0 copy-done.1
  17.1 0.0 copy-start
  17.1 0.0 copy-start.2
  17.1 0.0 copy-start.3
  17.1 0.0 copy-start.4
  17.1 3.5 %far.1.refs_8_ = bf16[256,128]{1,0:T(8,128)(2,1)S(1)} custom-call(bf16[8192,160]{1,0:T(8,128)(2,1)S(1)} %get-tuple-element.16.refs_0_, bf16[8192,160]{1,0:T(8,128)(2,1)S(1)} %get-tuple-element.23.refs_1_, bf16[320,128]{1,0:T(8,128)(2,1)S(1)} %add_convert_fusion.refs_4_.refs_2_.refs_0_, bf16[320,128]{1,0:T(8,128)(2,1)S(1)} %collective-permute-done.1.refs_3_.refs_1_, ...), custom_call_target="tpu_custom_call" | custom-call | flops 4294967296 | bytes 8388608 | tf_op jit(solution)/shard_map/far/pallas_call | solution.py:206
  20.6 1.6 %collective-permute-start.5 = (bf16[256,128]{1,0:T(8,128)(2,1)S(1)}, bf16[256,128]{1,0:T(8,128)(2,1)S(1)}, u32[]{:S(2)}, u32[]{:S(2)}) collective-permute-start(bf16[256,128]{1,0:T(8,128)(2,1)S(1)} %far.1.refs_8_), channel_id=1, source_target_pairs={{0,1},{1,0},{2,3},{3,2},{4,5},{5,4},{6,7},{7,6},{8,9},{9,8},{10,11... | collective-permute-start | bytes 196616 | tf_op jit(solution)/shard_map/ppermute | solution.py:25
  22.2 0.0 copy-done
  22.2 0.0 copy-done.2
  22.2 0.0 copy-done.3
  22.2 0.0 copy-done.4
  22.2 1.7 %own.1 = (f32[16,256]{1,0:T(8,128)S(1)}, f32[256,128]{1,0:T(8,128)S(1)}) custom-call(s32[1]{0:T(128)} %bitcast.member_ref, bf16[4096,160]{1,0:T(8,128)(2,1)S(1)} %get-tuple-element.24.count_ref, bf16[320,128]{1,0:T(8,128)(2,1)S(1)} %add_convert_fusion.refs_4_.refs_2_.refs_0_, bf16[320,128]{1,0:T(8,128)(2,1)S(1)} %collective-permute-done.1.refs_3_.refs_1_, ...), custom_call_target="tpu_custom_call" | custom-call | flops 1073741824 | bytes 2097152 | tf_op jit(solution)/shard_map/own/pallas_call | solution.py:281
  24.0 1.0 %collective-permute-done.5.far_ref = bf16[256,128]{1,0:T(8,128)(2,1)S(1)} collective-permute-done((bf16[256,128]{1,0:T(8,128)(2,1)S(1)}, bf16[256,128]{1,0:T(8,128)(2,1)S(1)}, u32[]{:S(2)}, u32[]{:S(2)}) %collective-permute-start.5) | collective-permute-done | bytes 65568 | tf_op jit(solution)/shard_map/ppermute | solution.py:25
  25.0 1.1 %other.1 = f32[16,512]{1,0:T(8,128)} custom-call(s32[1]{0:T(128)} %bitcast.member_ref, bf16[256,128]{1,0:T(8,128)(2,1)S(1)} %collective-permute-done.5.far_ref, f32[256,128]{1,0:T(8,128)S(1)} %get-tuple-element.25.moved_ref, bf16[512,16,128]{2,1,0:T(8,128)(2,1)S(1)} %copy-done, s32[1,512]{1,0:T(1,128)S(1)} %copy-done.4, f32[16,256]{1,0:T(8,128)S(1)} %get-tuple-element.26.own_ref), custom_call_target="tpu_custom_call" | custom-call | flops 268435456 | bytes 1048576 | tf_op jit(solution)/shard_map/other/pallas_call | solution.py:312
  (1 shorter events, 0.0 us)
Async XLA Ops:
  0.9 5.9 %collective-permute-start = (bf16[320,128]{1,0:T(8,128)(2,1)S(1)}, bf16[320,128]{1,0:T(8,128)(2,1)S(1)}, u32[]{:S(2)}, u32[]{:S(2)}) collective-permute-start(bf16[320,128]{1,0:T(8,128)(2,1)S(1)} %get-tuple-element.22), channel_id=1, source_target_pairs={{0,1},{1,0},{2,3},{3,2},{4,5},{5,4},{6,7},{7,6},{8,9},{9,8},{10,11... | collective-permute-start | bytes 245768 | tf_op jit(solution)/shard_map/ppermute | solution.py:25
  6.9 8.3 %collective-permute-start.1 = (bf16[320,128]{1,0:T(8,128)(2,1)S(1)}, bf16[320,128]{1,0:T(8,128)(2,1)S(1)}, u32[]{:S(2)}, u32[]{:S(2)}) collective-permute-start(bf16[320,128]{1,0:T(8,128)(2,1)S(1)} %add_convert_fusion.refs_4_.refs_2_.refs_0_), channel_id=1, source_target_pairs={{0,2},{2,0},{4,6},{6,4},{8,10},{10,8},{12,14},{14,12},{16,18},{18,... | collective-permute-start | bytes 245768 | tf_op jit(solution)/shard_map/ppermute | solution.py:29
  7.0 8.2 %collective-permute-start.2 = (bf16[320,128]{1,0:T(8,128)(2,1)S(1)}, bf16[320,128]{1,0:T(8,128)(2,1)S(1)}, u32[]{:S(2)}, u32[]{:S(2)}) collective-permute-start(bf16[320,128]{1,0:T(8,128)(2,1)S(1)} %add_convert_fusion.refs_4_.refs_2_.refs_0_), channel_id=1, source_target_pairs={{0,4},{2,6},{4,0},{6,2},{8,12},{10,14},{12,8},{14,10},{16,20},{18,... | collective-permute-start | bytes 245768 | tf_op jit(solution)/shard_map/ppermute | solution.py:29
  8.6 6.6 %collective-permute-start.3 = (bf16[320,128]{1,0:T(8,128)(2,1)S(1)}, bf16[320,128]{1,0:T(8,128)(2,1)S(1)}, u32[]{:S(2)}, u32[]{:S(2)}) collective-permute-start(bf16[320,128]{1,0:T(8,128)(2,1)S(1)} %add_convert_fusion.refs_4_.refs_2_.refs_0_), channel_id=1, source_target_pairs={{0,8},{2,10},{4,12},{6,14},{8,0},{10,2},{12,4},{14,6},{16,24},{18,... | collective-permute-start | bytes 245768 | tf_op jit(solution)/shard_map/ppermute | solution.py:29
  10.2 6.9 %collective-permute-start.4 = (bf16[320,128]{1,0:T(8,128)(2,1)S(1)}, bf16[320,128]{1,0:T(8,128)(2,1)S(1)}, u32[]{:S(2)}, u32[]{:S(2)}) collective-permute-start(bf16[320,128]{1,0:T(8,128)(2,1)S(1)} %add_convert_fusion.refs_4_.refs_2_.refs_0_), channel_id=1, source_target_pairs={{0,16},{2,18},{4,20},{6,22},{8,24},{10,26},{12,28},{14,30},{16,0},... | collective-permute-start | bytes 245768 | tf_op jit(solution)/shard_map/ppermute | solution.py:29
  12.7 4.3 %copy-start.1 = (bf16[64,128,128]{2,1,0:T(8,128)(2,1)S(1)}, bf16[64,128,128]{2,1,0:T(8,128)(2,1)}, u32[]{:S(2)}) copy-start(bf16[64,128,128]{2,1,0:T(8,128)(2,1)} %param.18) | copy-start | bytes 6291460
  17.1 5.1 %copy-start = (bf16[512,16,128]{2,1,0:T(8,128)(2,1)S(1)}, bf16[512,16,128]{2,1,0:T(8,128)(2,1)}, u32[]{:S(2)}) copy-start(bf16[512,16,128]{2,1,0:T(8,128)(2,1)} %basis_ref.1) | copy-start | bytes 6291460
  17.1 5.1 %copy-start.2 = (bf16[8,128,128]{2,1,0:T(8,128)(2,1)S(1)}, bf16[8,128,128]{2,1,0:T(8,128)(2,1)}, u32[]{:S(2)}) copy-start(bf16[8,128,128]{2,1,0:T(8,128)(2,1)} %refs_7_.1) | copy-start | bytes 786436
  17.1 5.1 %copy-start.3 = (f32[64,128]{1,0:T(8,128)S(1)}, f32[64,128]{1,0:T(8,128)}, u32[]{:S(2)}) copy-start(f32[64,128]{1,0:T(8,128)} %refs_6_.1) | copy-start | bytes 98308
  17.1 5.1 %copy-start.4 = (s32[1,512]{1,0:T(1,128)S(1)}, s32[1,512]{1,0:T(1,128)}, u32[]{:S(2)}) copy-start(s32[1,512]{1,0:T(1,128)} %counts_ref.1) | copy-start | bytes 6148
  20.6 4.3 %collective-permute-start.5 = (bf16[256,128]{1,0:T(8,128)(2,1)S(1)}, bf16[256,128]{1,0:T(8,128)(2,1)S(1)}, u32[]{:S(2)}, u32[]{:S(2)}) collective-permute-start(bf16[256,128]{1,0:T(8,128)(2,1)S(1)} %far.1.refs_8_), channel_id=1, source_target_pairs={{0,1},{1,0},{2,3},{3,2},{4,5},{5,4},{6,7},{7,6},{8,9},{9,8},{10,11... | collective-permute-start | bytes 196616 | tf_op jit(solution)/shard_map/ppermute | solution.py:25
